TPU v7x, 256 devices: a whole 4x4x8 slice. The times are simulated.
256 devices in a mesh: dp: 8 (over y, x_hi), ctx: 32 (over x_lo, z, core).
Axes of the slice: x: 4 (x_hi: 2, x_lo: 2; x = x_hi * 2 + x_lo), y: 4, z: 8, core: 2. Of those that a mesh axis runs over, the one named last changes fastest.
Arguments:
- inputs: bfloat16 [8, 64, 65536], P('dp', None, 'ctx'), may hold values from -6 to 6
- out_grad: bfloat16 [8, 64, 65536], P('dp', None, 'ctx'), may hold values from -0.0390625 to 0.0390625
- master: float32 [64, 65536], P('ctx', 'dp'), may hold values from -0.0234375 to 0.0234375
- moment_one: float32 [64, 65536], P('ctx', 'dp'), may hold values from -6 to 6
- moment_two: float32 [64, 65536], P('ctx', 'dp'), may hold values from 0.05 to 1
- next_inputs: bfloat16 [8, 64, 65536], P('dp', None, 'ctx'), may hold values from -6 to 6
Outputs:
- new_master: float32 [64, 65536], P('ctx', 'dp')
- new_moment_one: float32 [64, 65536], P('ctx', 'dp')
- new_moment_two: float32 [64, 65536], P('ctx', 'dp')
- next_out: bfloat16 [8, 64, 65536], P('dp', None, 'ctx')
All inputs are finite; a program needn't handle non-finite values.
Results may differ from a plain program's by a relative error of at most 0.007.
Values may be sent and summed in bfloat16 or wider, within the bound.
No kernel may reach another device: no remote copies, remote signals or barrier semaphores. Data moves between devices by JAX's collectives and lax.ppermute only.
A program may use at most 128 MiB of HBM per device.

v0:
```python
import math

import jax
import jax.numpy as jnp
from jax import lax
from jax.sharding import PartitionSpec as P

FA = 256


precise = lax.Precision.HIGH


def angles(rows, cols, period, row_start, col_start):
    row_ids = lax.broadcasted_iota(jnp.int32, (rows, cols), 0) + row_start
    col_ids = lax.broadcasted_iota(jnp.int32, (rows, cols), 1) + col_start
    phase = (row_ids * col_ids % period).astype(jnp.float32) * (2.0 * math.pi / period)
    return (jnp.cos(phase), jnp.sin(phase))


def mult(form, left, right):
    return jnp.einsum(form, left, right, precision=precise, preferred_element_type=jnp.float32)


def first_section(values, row_start, longer):
    cosine, sine = angles(longer, values.shape[1], longer, 0, row_start)
    real = mult("kr,crn->ckn", cosine, values)
    imag = -mult("kr,crn->ckn", sine, values)
    return (real, imag)


def second_section(real, imag):
    longer, inner = (real.shape[1], real.shape[2])
    tw_cos, tw_sin = angles(longer, inner, longer * inner, 0, 0)
    turned_re = real * tw_cos + imag * tw_sin
    turned_im = imag * tw_cos - real * tw_sin
    cosine, sine = angles(inner, inner, inner, 0, 0)
    out_re = mult("ckn,nm->ckm", turned_re, cosine) + mult("ckn,nm->ckm", turned_im, sine)
    out_im = mult("ckn,nm->ckm", turned_im, cosine) - mult("ckn,nm->ckm", turned_re, sine)
    return (out_re, out_im)


def back_section(spec_re, spec_im):
    longer, inner = (spec_re.shape[1], spec_re.shape[2])
    cosine, sine = angles(inner, inner, inner, 0, 0)
    mixed_re = mult("ckm,mn->ckn", spec_re, cosine) - mult("ckm,mn->ckn", spec_im, sine)
    mixed_im = mult("ckm,mn->ckn", spec_re, sine) + mult("ckm,mn->ckn", spec_im, cosine)
    tw_cos, tw_sin = angles(longer, inner, longer * inner, 0, 0)
    return (mixed_re * tw_cos - mixed_im * tw_sin, mixed_re * tw_sin + mixed_im * tw_cos)


def last_rows(back_re, back_im, start, count, form):
    longer, inner = (back_re.shape[1], back_re.shape[2])
    cosine, sine = angles(count, longer, longer, start, 0)
    total = mult(form, cosine, back_re) - mult(form, sine, back_im)
    return total * (1.0 / (longer * inner))


def spectrum(block, inner):
    channels, length = (block.shape[1], block.shape[2])
    values = block[0].reshape(channels, length // inner, inner)
    real, imag = first_section(values, 0, 2 * (length // inner))
    return second_section(real, imag)


def regroup_next(next_inputs):
    return lax.all_to_all(next_inputs, "ctx", split_axis=1, concat_axis=2, tiled=True)


def local(inputs, out_grad, master, moment_one, moment_two, next_inputs):
    inner = FA
    seq_local, grad_local = (
        lax.all_to_all(inputs, "ctx", split_axis=1, concat_axis=2, tiled=True),
        lax.all_to_all(out_grad, "ctx", split_axis=1, concat_axis=2, tiled=True),
    )
    channels, length = (seq_local.shape[1], seq_local.shape[2])
    half_rows = length // inner
    longer = 2 * half_rows
    seq_re, seq_im = spectrum(seq_local, inner)
    grad_re, grad_im = spectrum(grad_local, inner)
    prod_re = seq_re * grad_re + seq_im * grad_im
    prod_im = seq_re * grad_im - seq_im * grad_re
    back_re, back_im = back_section(prod_re, prod_im)
    rows_own = half_rows // lax.axis_size("dp")
    summed = lax.psum_scatter(
        last_rows(
            back_re, back_im, jnp.int32(0), lax.axis_size("dp") * rows_own, "rk,ckn->rcn"
        ).astype(jnp.bfloat16),
        "dp",
        scatter_dimension=0,
        tiled=True,
    ).astype(jnp.float32)
    grad = jnp.transpose(summed, (1, 0, 2)).reshape(channels, rows_own * inner)
    new_one = 0.9 * moment_one + 0.1 * grad
    new_two = 0.999 * moment_two + 0.001 * grad * grad
    first_hat = new_one / (1.0 - 0.9**10)
    second_hat = new_two / (1.0 - 0.999**10)
    new_master = master - 0.01 * (first_hat / (jnp.sqrt(second_hat) + 1e-08) + 0.1 * master)
    filters = new_master.astype(jnp.bfloat16).reshape(channels, rows_own, inner)
    part_re, part_im = first_section(
        lax.all_gather(filters, "dp", axis=1, tiled=True), jnp.int32(0), longer
    )
    filt_re, filt_im = second_section(part_re, part_im)
    next_local = regroup_next(next_inputs)
    next_re, next_im = spectrum(next_local, inner)
    out_re = next_re * filt_re - next_im * filt_im
    out_im = next_re * filt_im + next_im * filt_re
    final_re, final_im = back_section(out_re, out_im)
    result = last_rows(final_re, final_im, 0, half_rows, "rk,ckn->crn")
    result = result.reshape(1, channels, length).astype(jnp.bfloat16)
    next_out = lax.all_to_all(result, "ctx", split_axis=2, concat_axis=1, tiled=True)
    return (new_master, new_one, new_two, next_out)


def solution(mesh):
    return jax.shard_map(
        local,
        mesh=mesh,
        in_specs=(
            P("dp", None, "ctx"),
            P("dp", None, "ctx"),
            P("ctx", "dp"),
            P("ctx", "dp"),
            P("ctx", "dp"),
            P("dp", None, "ctx"),
        ),
        out_specs=(P("ctx", "dp"), P("ctx", "dp"), P("ctx", "dp"), P("dp", None, "ctx")),
        check_vma=False,
    )
```

profile of v0, /device:TPU:1, one launch (start us, length us, event | category | flops | bytes accessed | tf_op | source)
XLA Modules:
  0.0 822.5 jit_solution(4958300976924144988)
XLA Ops:
  9.1 2.1 reduce.8
  12.1 11.0 %all-to-all-start.2 = ((bf16[32,2,2048]{2,1,0:T(2,128)(2,1)}), bf16[32,2,2048]{2,1,0:T(2,128)(2,1)S(1)}, u32[]{:S(2)}, u32[]{:S(2)}) async-start(bf16[32,2,2048]{2,1,0:T(2,128)(2,1)} %reshape.80), calls=%async_computation.3 | async-start | bytes 524288 | tf_op jit(solution)/shard_map/all_to_all | solution.py:67
  24.5 2.1 reduce.7
  28.9 2.1 reduce.6
  31.9 2.1 fusion.113
  34.7 8.2 all-to-all-start.1
  45.7 2.3 convolution_negate_fusion.1
  48.0 3.2 fusion.52
  51.2 3.1 all-to-all-done.1
  54.3 6.0 all-to-all-start
  61.3 2.5 bitcast_reduce_fusion.1
  66.6 4.2 convolution_negate_fusion.2
  70.8 4.2 fusion.54
  75.0 2.9 reshape.77
  78.0 2.5 bitcast_reduce_fusion.2
  83.2 3.2 convolution_negate_fusion.3
  86.5 3.2 fusion.56
  89.7 3.1 fusion.12
  92.8 3.1 fusion.16
  96.0 1.6 fusion.18
  97.6 1.8 fusion.22
  99.5 3.1 convolution_subtract_fusion.4
  102.6 3.1 convolution_add_fusion.4
  105.7 1.6 convolution_add_fusion.5
  107.4 1.8 multiply_subtract_fusion.3
  112.3 2.0 convolution_add_fusion.3
  115.9 2.6 fusion.34
  118.5 3.3 fusion.4
  121.9 2.6 fusion.6
  124.5 1.6 fusion.10
  126.1 2.8 convolution_add_fusion.2
  128.9 67.8 %reduce-scatter.2.cloned.1.call-done = bf16[32,2,256]{2,0,1:T(8,128)(2,1)} async-done(((bf16[256,2,256]{2,0,1:T(8,128)(2,1)}), bf16[32,2,256]{2,0,1:T(8,128)(2,1)}) %reduce-scatter.2.cloned.1.call-update) | async-done | bytes 32784 | tf_op jit(solution)/shard_map/reduce_scatter | solution.py:85
  198.4 28.6 %all_gather.3 = bf16[2,256,256]{2,1,0:T(8,128)(2,1)S(1)} all-gather(bf16[2,32,256]{2,1,0:T(8,128)(2,1)S(1)} %bitcast.192), channel_id=1, replica_groups=mesh['dp'=8,'ctx'=32] {'dp'}, dimensions={1}, use_global_device_ids=true | all-gather | bytes 294912 | tf_op jit(solution)/shard_map/all_gather | solution.py:101
  227.0 2.3 fusion
  229.3 2.3 convolution_bitcast_fusion
  231.6 1.7 fusion.98
  233.2 1.7 fusion.101
  234.9 1.7 convolution_subtract_fusion.1
  236.6 1.7 convolution_add_fusion.1
  238.2 3.7 multiply_add_fusion
  248.2 2.8 fusion.27
  251.0 3.0 fusion.5
  254.2 50.3 %copy.63 = bf16[1,2,65536]{1,0,2:T(2,128)(2,1)} copy(bf16[1,2,65536]{2,1,0:T(2,128)(2,1)S(1)} %convert_element_type.177) | data formatting | bytes 524288 | tf_op jit(solution)/shard_map/convert_element_type | solution.py:110
  304.5 355.8 %reduce.9 = bf16[65536,2]{1,0:T(8,128)(2,1)} reduce(bf16[65536,1,2]{2,1,0:T(2,128)(2,1)} %bitcast.181, bf16[]{:T(256)} %broadcast.385), dimensions={1}, to_apply=%bitcast.143.reduce_sub_computation | reduce | bytes 524290
  660.3 25.0 %reshape.82 = bf16[32,2,2048]{2,1,0:T(2,128)(2,1)S(1)} reshape(bf16[65536,2]{1,0:T(8,128)(2,1)} %reduce.9) | data formatting | bytes 524288
  685.3 27.6 %all_to_all.63 = bf16[32,2,2048]{2,1,0:T(2,128)(2,1)S(1)} all-to-all(bf16[32,2,2048]{2,1,0:T(2,128)(2,1)S(1)} %reshape.82), channel_id=1, replica_groups=mesh['dp'=8,'ctx'=32] {'ctx'}, dimensions={0} | all-to-all | bytes 524288 | tf_op jit(solution)/shard_map/all_to_all | solution.py:111
  712.8 40.6 %reshape.83 = bf16[65536,1,2]{2,1,0:T(2,128)(2,1)} reshape(bf16[32,2,2048]{2,1,0:T(2,128)(2,1)S(1)} %all_to_all.63) | data formatting | bytes 524288
  753.4 60.8 %copy.64 = bf16[1,2,65536]{2,1,0:T(2,128)(2,1)S(1)} copy(bf16[1,2,65536]{1,0,2:T(2,128)(2,1)} %bitcast.182) | data formatting | bytes 524288 | tf_op jit(solution)/shard_map/all_to_all | solution.py:111
  (47 shorter events, 31.3 us)
Async XLA Ops:
  12.1 22.6 %all-to-all-start.2 = ((bf16[32,2,2048]{2,1,0:T(2,128)(2,1)}), bf16[32,2,2048]{2,1,0:T(2,128)(2,1)S(1)}, u32[]{:S(2)}, u32[]{:S(2)}) async-start(bf16[32,2,2048]{2,1,0:T(2,128)(2,1)} %reshape.80), calls=%async_computation.3 | async-start | bytes 524288 | tf_op jit(solution)/shard_map/all_to_all | solution.py:67
  34.7 19.6 %all-to-all-start.1 = ((bf16[32,2,2048]{2,1,0:T(2,128)(2,1)}), bf16[32,2,2048]{2,1,0:T(2,128)(2,1)S(1)}, u32[]{:S(2)}, u32[]{:S(2)}) async-start(bf16[32,2,2048]{2,1,0:T(2,128)(2,1)} %reshape.78), calls=%async_computation.1 | async-start | bytes 524288 | tf_op jit(solution)/shard_map/all_to_all | solution.py:74
  45.0 0.7 copy-start
  54.3 20.7 %all-to-all-start = ((bf16[32,2,2048]{2,1,0:T(2,128)(2,1)}), bf16[32,2,2048]{2,1,0:T(2,128)(2,1)}, u32[]{:S(2)}, u32[]{:S(2)}) async-start(bf16[32,2,2048]{2,1,0:T(2,128)(2,1)} %reshape.76), calls=%async_computation | async-start | bytes 524288 | tf_op jit(solution)/shard_map/all_to_all | solution.py:73
  60.3 136.4 %reduce-scatter.2.cloned.1.call-start = ((), (), s32[]{:S(2)}) async-start(), calls=%async_computation.5 | async-start | bytes 294912 | tf_op jit(solution)/shard_map/reduce_scatter | solution.py:85
  95.9 101.6 %copy-start.1 = (f32[2,8192]{1,0:T(2,128)S(1)}, f32[2,8192]{1,0:T(2,128)}, u32[]{:S(2)}) copy-start(f32[2,8192]{1,0:T(2,128)} %param.8) | copy-start | bytes 196612
  96.0 101.6 %copy-start.2 = (f32[2,8192]{1,0:T(2,128)S(1)}, f32[2,8192]{1,0:T(2,128)}, u32[]{:S(2)}) copy-start(f32[2,8192]{1,0:T(2,128)} %param.9) | copy-start | bytes 196612
  96.0 101.6 %copy-start.3 = (f32[2,8192]{1,0:T(2,128)S(1)}, f32[2,8192]{1,0:T(2,128)}, u32[]{:S(2)}) copy-start(f32[2,8192]{1,0:T(2,128)} %param.10) | copy-start | bytes 196612
Sparse Core Ops, SparseCore 0:
  122.0 74.6 reduce-scatter.1
where the time goes:
time: 832 us; the launch traced here: 822 us
  other arithmetic  366 us (44%)
  local copies, waits for them, and re-layouts  203 us (24%)
  matrix products  86.3 us (10%)
  waiting for transfers between devices  71.7 us (9%)
  blocking collectives  56.1 us (7%)
  starting transfers between devices  25.3 us (3%)
  between operations  14.7 us (2%)
    unnamed x5, other arithmetic  363 us
    dot_general x36, matrix products, mult(): jnp.einsum(form, left, right, precision=precise, preferred_element_type=j...  86.3 us
    unnamed x23, local copies, waits for them, and re-layouts  77.9 us
    reduce_scatter x1, waiting for transfers between devices, local(): lax.psum_scatter(last_rows(back_re, back_im, jnp.int32(0), lax.axis_size(...  67.8 us
    all_to_all x3, local copies, waits for them, and re-layouts, local(): lax.all_to_all(result, 'ctx', split_axis=2, concat_axis=1, tiled=True)  61.9 us
    convert_element_type x3, local copies, waits for them, and re-layouts, local(): result = result.reshape(1, channels, length).astype(jnp.bfloat16)  50.5 us
    all_gather x1, blocking collectives, local(): lax.all_gather(filters, 'dp', axis=1, tiled=True)  28.6 us
    all_to_all x1, blocking collectives, local(): lax.all_to_all(result, 'ctx', split_axis=2, concat_axis=1, tiled=True)  27.6 us
  transfers between devices with their start and end apart: 4, of which 3 were waited for; matrix products, arithmetic and copies ran while one was open for 5% of the time, Pallas kernels for 0%

commit v1 on v0

v1 whole, which is shorter than its diff:
```python
import math

import jax
import jax.numpy as jnp
import numpy as np
from jax import lax
from jax.experimental import pallas as pl
from jax.experimental.pallas import tpu as pltpu
from jax.sharding import PartitionSpec as P

ROWS = 512
LANES = 128
BLOCK = 128

f32 = jnp.float32
bf16 = jnp.bfloat16


def split_table(values):
    high = values.astype(bf16)
    low = (values - high.astype(np.float64)).astype(bf16)
    return high, low


def tables():
    half = np.arange(ROWS) + 0.5
    lanes = np.arange(LANES)
    outer = 2.0 * math.pi * np.outer(half, half) / (2 * ROWS)
    long_side = np.concatenate([np.cos(outer), np.sin(outer)], axis=1)
    turn = 2.0 * math.pi * np.outer(half, lanes / (2.0 * ROWS * LANES) - 1.0 / (4 * ROWS))
    twiddle = np.concatenate([np.cos(turn), np.sin(turn)], axis=1).astype(np.float32)
    inner = 2.0 * math.pi * (np.outer(lanes, lanes) % LANES) / LANES
    cosine, sine = np.cos(inner), np.sin(inner)
    short = np.block([[cosine, sine], [-sine, cosine]])
    short_hi, short_lo = split_table(short)
    long_hi, long_lo = split_table(long_side)
    return (long_hi, long_lo, twiddle, short_hi, short_lo, short_hi.T.copy(), short_lo.T.copy())


def dot(left, right):
    return jnp.dot(left, right, preferred_element_type=f32)


def halves(values):
    high = values.astype(bf16)
    return high, (values - high.astype(f32)).astype(bf16)


def times_short(values, hi_ref, lo_ref):
    high, low = halves(values)
    rows = values.shape[0]
    both = dot(jnp.concatenate([high, low], axis=0), hi_ref[...])
    return both[:rows] + both[rows:] + dot(high, lo_ref[...])


def forward_block(start, waves, long_hi, long_lo, twiddle, short_hi, short_lo):
    rows = pl.ds(start, BLOCK)
    left = jnp.concatenate(
        [long_hi[rows, :ROWS], long_hi[rows, ROWS:], long_lo[rows, :ROWS], long_lo[rows, ROWS:]], axis=0
    )
    cosine, sine = twiddle[rows, :LANES], twiddle[rows, LANES:]
    turned = []
    for wave in waves:
        first = dot(left, wave)
        first = first[: 2 * BLOCK] + first[2 * BLOCK :]
        for c in range(wave.shape[1] // LANES):
            real = first[:BLOCK, c * LANES : (c + 1) * LANES]
            imag = first[BLOCK:, c * LANES : (c + 1) * LANES]
            turned.append(
                jnp.concatenate([real * cosine - imag * sine, real * sine + imag * cosine], axis=1)
            )
    spectra = times_short(jnp.concatenate(turned, axis=0), short_hi, short_lo)
    return [spectra[i * BLOCK : (i + 1) * BLOCK] for i in range(len(turned))]


def backward_block(start, products, twiddle, back_hi, back_lo, high_ref, low_ref):
    rows = pl.ds(start, BLOCK)
    cosine, sine = twiddle[rows, :LANES], twiddle[rows, LANES:]
    mixed = times_short(jnp.concatenate(products, axis=0), back_hi, back_lo)
    for c in range(len(products)):
        real = mixed[c * BLOCK : (c + 1) * BLOCK, :LANES]
        imag = mixed[c * BLOCK : (c + 1) * BLOCK, LANES:]
        lanes = slice(c * LANES, (c + 1) * LANES)
        for at, part in ((start, real * cosine + imag * sine), (ROWS + start, imag * cosine - real * sine)):
            high, low = halves(part)
            high_ref[pl.ds(at, BLOCK), lanes] = high
            low_ref[pl.ds(at, BLOCK), lanes] = low


def last_stage(long_hi, long_lo, high_ref, low_ref):
    left = jnp.concatenate([long_hi[...], long_lo[...]], axis=0)
    both = dot(left, high_ref[...])
    total = both[:ROWS] + both[ROWS:] + dot(long_hi[...], low_ref[...])
    return total * (1.0 / (ROWS * LANES))


def wave_of(ref, first):
    parts = [ref[:, first + c].reshape(ROWS, LANES) for c in range(2)]
    return jnp.concatenate(parts, axis=1)


def pack_body(*refs):
    count = len(refs) // 2 - 1 + len(refs) % 2
    sources, out_ref, scratch = refs[:count], refs[count], refs[count + 1 :]
    for i, ref in enumerate(sources):
        values = ref[...].astype(f32)
        channels, length = values.shape
        pieces = length // LANES
        for k in range(pieces):
            scratch[i][pl.ds(k, channels, stride=pieces), :] = values[:, k * LANES : (k + 1) * LANES]
        peers = out_ref.shape[0]
        out_ref[:, 2 * i : 2 * i + 2] = scratch[i][...].reshape(peers, 2, pieces, LANES).astype(bf16)


def unpack_body(in_ref, out_ref, scratch):
    channels, length = out_ref.shape
    pieces = length // LANES
    scratch[...] = in_ref[...].astype(f32).reshape(channels * pieces, LANES)
    for k in range(pieces):
        out_ref[:, k * LANES : (k + 1) * LANES] = scratch[pl.ds(k, channels, stride=pieces), :].astype(bf16)


def correlate_body(
    in_ref, long_hi, long_lo, twiddle, short_hi, short_lo, back_hi, back_lo, out_ref, high_ref, low_ref, scratch
):
    seq, grad = wave_of(in_ref, 0), wave_of(in_ref, 2)

    def step(b, carry):
        start = pl.multiple_of(b * BLOCK, BLOCK)
        spectra = forward_block(start, (seq, grad), long_hi, long_lo, twiddle, short_hi, short_lo)
        products = []
        for c in range(2):
            s_re, s_im = spectra[c][:, :LANES], spectra[c][:, LANES:]
            g_re, g_im = spectra[2 + c][:, :LANES], spectra[2 + c][:, LANES:]
            products.append(
                jnp.concatenate([g_re * s_re + g_im * s_im, g_im * s_re - g_re * s_im], axis=1)
            )
        backward_block(start, products, twiddle, back_hi, back_lo, high_ref, low_ref)
        return carry

    lax.fori_loop(0, ROWS // BLOCK, step, 0)
    result = last_stage(long_hi, long_lo, high_ref, low_ref)
    for c in range(2):
        scratch[pl.ds(c, ROWS, stride=2), :] = result[:, c * LANES : (c + 1) * LANES]
    out_ref[...] = scratch[...].astype(bf16).reshape(out_ref.shape)


def adam_body(grad_ref, master, one, two, new_master, new_one, new_two, filters):
    grad = grad_ref[0].astype(f32)
    for q in range(1, grad_ref.shape[0]):
        grad = grad + grad_ref[q].astype(f32)
    first = 0.9 * one[...] + 0.1 * grad
    second = 0.999 * two[...] + 0.001 * grad * grad
    new_one[...] = first
    new_two[...] = second
    first_hat = first / (1.0 - 0.9**10)
    second_hat = second / (1.0 - 0.999**10)
    old = master[...]
    new = old - 0.01 * (first_hat / (jnp.sqrt(second_hat) + 1e-08) + 0.1 * old)
    new_master[...] = new
    rounded = new.astype(bf16)
    for q in range(filters.shape[0]):
        filters[q] = rounded


def spectrum_body(in_ref, long_hi, long_lo, twiddle, short_hi, short_lo, out_ref):
    wave = wave_of(in_ref, 0)

    def step(b, carry):
        start = pl.multiple_of(b * BLOCK, BLOCK)
        spectra = forward_block(start, (wave,), long_hi, long_lo, twiddle, short_hi, short_lo)
        for c in range(2):
            out_ref[c, pl.ds(start, BLOCK), :] = spectra[c]
        return carry

    lax.fori_loop(0, ROWS // BLOCK, step, 0)


def convolve_body(
    in_ref, next_ref, long_hi, long_lo, twiddle, short_hi, short_lo, back_hi, back_lo,
    out_ref, high_ref, low_ref, scratch,
):
    scratch[...] = in_ref[...].reshape(2 * ROWS, LANES).astype(f32)
    wave = jnp.concatenate(
        [scratch[pl.ds(c, ROWS, stride=2), :].astype(bf16) for c in range(2)], axis=1
    )

    def step(b, carry):
        start = pl.multiple_of(b * BLOCK, BLOCK)
        spectra = forward_block(start, (wave,), long_hi, long_lo, twiddle, short_hi, short_lo)
        products = []
        for c in range(2):
            f_re, f_im = spectra[c][:, :LANES], spectra[c][:, LANES:]
            n_re = next_ref[c, pl.ds(start, BLOCK), :LANES]
            n_im = next_ref[c, pl.ds(start, BLOCK), LANES:]
            products.append(
                jnp.concatenate([f_re * n_re - f_im * n_im, f_re * n_im + f_im * n_re], axis=1)
            )
        backward_block(start, products, twiddle, back_hi, back_lo, high_ref, low_ref)
        return carry

    lax.fori_loop(0, ROWS // BLOCK, step, 0)
    result = last_stage(long_hi, long_lo, high_ref, low_ref).astype(bf16)
    peers, pieces = out_ref.shape[0], out_ref.shape[2]
    for c in range(2):
        out_ref[:, c] = result[:, c * LANES : (c + 1) * LANES].reshape(peers, pieces, LANES)


def call(body, name, out_shape, scratch, *args):
    return pl.pallas_call(
        body,
        out_shape=out_shape,
        in_specs=[pl.BlockSpec(memory_space=pltpu.VMEM)] * len(args),
        out_specs=jax.tree.map(lambda _: pl.BlockSpec(memory_space=pltpu.VMEM), out_shape),
        scratch_shapes=scratch,
        name=name,
    )(*args)


def shape(dims, dtype):
    return jax.ShapeDtypeStruct(dims, dtype)


def interleave(values):
    channels, taps = values.shape
    pieces = taps // LANES
    return values.reshape(channels, pieces, LANES).transpose(1, 0, 2).reshape(channels * pieces, LANES)


def deinterleave(values, channels):
    pieces = values.shape[0] // channels
    return values.reshape(pieces, channels, LANES).transpose(1, 0, 2).reshape(channels, pieces * LANES)


def exchange(values, axis):
    return lax.all_to_all(values, axis, split_axis=0, concat_axis=0, tiled=True)


def local(inputs, out_grad, master, moment_one, moment_two, next_inputs):
    channels, length = inputs.shape[1:]
    peers = lax.axis_size("ctx")
    owners = lax.axis_size("dp")
    pieces = length // LANES
    rows = channels * pieces
    long_hi, long_lo, twiddle, short_hi, short_lo, back_hi, back_lo = (jnp.asarray(t) for t in tables())
    ahead = (long_hi, long_lo, twiddle, short_hi, short_lo)
    work = [pltpu.VMEM((2 * ROWS, 2 * LANES), bf16)] * 2 + [pltpu.VMEM((2 * ROWS, LANES), f32)]

    packed = call(
        pack_body, "pack", shape((peers, 4, pieces, LANES), bf16), [pltpu.VMEM((rows, LANES), f32)] * 2,
        inputs[0], out_grad[0],
    )
    next_packed = call(
        pack_body, "pack_next", shape((peers, 2, pieces, LANES), bf16), [pltpu.VMEM((rows, LANES), f32)],
        next_inputs[0],
    )
    partial = call(
        correlate_body, "correlate", shape((owners, 2 * ROWS // owners, LANES), bf16), work,
        exchange(packed, "ctx"), *ahead, back_hi, back_lo,
    )
    partials = exchange(partial, "dp")
    own = shape((2 * ROWS // owners, LANES), f32)
    new_master, new_one, new_two, filters = call(
        adam_body, "adam", (own, own, own, shape(partial.shape, bf16)), [],
        partials, interleave(master), interleave(moment_one), interleave(moment_two),
    )
    next_spectrum = call(
        spectrum_body, "spectrum", shape((2, ROWS, 2 * LANES), f32), [], exchange(next_packed, "ctx"), *ahead
    )
    result = call(
        convolve_body, "convolve", shape((peers, 2, pieces, LANES), bf16), work,
        exchange(filters, "dp"), next_spectrum, *ahead, back_hi, back_lo,
    )
    next_out = call(
        unpack_body, "unpack", shape((channels, length), bf16), [pltpu.VMEM((rows, LANES), f32)],
        exchange(result, "ctx"),
    )
    return (deinterleave(new_master, 2), deinterleave(new_one, 2), deinterleave(new_two, 2), next_out[None])


def solution(mesh):
    return jax.shard_map(
        local,
        mesh=mesh,
        in_specs=(
            P("dp", None, "ctx"),
            P("dp", None, "ctx"),
            P("ctx", "dp"),
            P("ctx", "dp"),
            P("ctx", "dp"),
            P("dp", None, "ctx"),
        ),
        out_specs=(P("ctx", "dp"), P("ctx", "dp"), P("ctx", "dp"), P("dp", None, "ctx")),
        check_vma=False,
    )
```

time: 832 us -> 114 us (0.14); the launches traced: 822 us -> 114 us
  other arithmetic: 366 us -> 0 us
  local copies, waits for them, and re-layouts: 203 us -> 2.11 us
  matrix products: 86.3 us -> 0 us
  waiting for transfers between devices: 71.7 us -> 17.9 us
  Pallas kernels: 0 us -> 29.8 us
  between operations: 14.7 us -> 0.66 us
  blocking collectives: 56.1 us -> 46.6 us
  starting transfers between devices: 25.3 us -> 16.7 us
    unnamed x5 -> x0, other arithmetic: 363 us -> none
    dot_general x36 -> x0, matrix products: 86.3 us -> none  [mult(): jnp.einsum(form, left, right, precision=precise, preferred_element_type=j...]
    unnamed x23 -> x6, local copies, waits for them, and re-layouts: 77.9 us -> 2.11 us
    all_to_all x12 -> x0, local copies, waits for them, and re-layouts: 72.5 us -> none  [the longest x3 61.9 us: local(): lax.all_to_all(result, 'ctx', split_axis=2, concat_axis=1, tiled=True)]
    reduce_scatter x1 -> x0, waiting for transfers between devices: 67.8 us -> none  [local(): lax.psum_scatter(last_rows(back_re, back_im, jnp.int32(0), lax.axis_size(...]
    convert_element_type x3 -> x0, local copies, waits for them, and re-layouts: 50.5 us -> none  [local(): result = result.reshape(1, channels, length).astype(jnp.bfloat16)]
    pallas_call x0 -> x7, Pallas kernels: none -> 29.8 us  [call(): pl.pallas_call(body, out_shape=out_shape, in_specs=[pl.BlockSpec(memory_s...]
    all_gather x1 -> x0, blocking collectives: 28.6 us -> none  [local(): lax.all_gather(filters, 'dp', axis=1, tiled=True)]
  transfers between devices with their start and end apart: 4 -> 3, of which waited for: 3 -> 3; matrix products, arithmetic and copies ran while one was open for 5% -> 0% of each run, Pallas kernels for 0% -> 8%
where the time goes in v1:
time: 114 us
  blocking collectives  46.6 us (41%)
  Pallas kernels  29.8 us (26%)
  waiting for transfers between devices  17.9 us (16%)
  starting transfers between devices  16.7 us (15%)
  local copies, waits for them, and re-layouts  2.11 us (2%)
    all_to_all x2, blocking collectives, exchange(): return lax.all_to_all(values, axis, split_axis=0, concat_axis=0, tiled=True)  46.6 us
    pallas_call x7, Pallas kernels, call(): pl.pallas_call(body, out_shape=out_shape, in_specs=[pl.BlockSpec(memory_s...  29.8 us
    all_to_all x3, waiting for transfers between devices, exchange(): return lax.all_to_all(values, axis, split_axis=0, concat_axis=0, tiled=True)  17.9 us
    all_to_all x3, starting transfers between devices, exchange(): return lax.all_to_all(values, axis, split_axis=0, concat_axis=0, tiled=True)  16.7 us
  transfers between devices with their start and end apart: 3, of which 3 were waited for; matrix products, arithmetic and copies ran while one was open for 0% of the time, Pallas kernels for 8%

profile of v1, /device:TPU:1, one launch (start us, length us, event | category | flops | bytes accessed | tf_op | source)
XLA Modules:
  0.0 113.8 jit_solution(5368933052831631691)
XLA Ops:
  0.6 2.2 %pack.1 = bf16[32,4,16,128]{3,2,1,0:T(8,128)(2,1)} custom-call(bf16[64,2048]{1,0:T(8,128)(2,1)} %bitcast.36, bf16[64,2048]{1,0:T(8,128)(2,1)} %bitcast.37), custom_call_target="tpu_custom_call" | custom-call | tf_op jit(solution)/shard_map/pack/pallas_call | solution.py:210
  2.8 27.7 %all_to_all.25.in_ref = bf16[32,4,16,128]{3,2,1,0:T(8,128)(2,1)} all-to-all(bf16[32,4,16,128]{3,2,1,0:T(8,128)(2,1)} %pack.1), channel_id=1, replica_groups=mesh['dp'=8,'ctx'=32] {'ctx'}, dimensions={0} | all-to-all | bytes 1048576 | tf_op jit(solution)/shard_map/all_to_all | solution.py:236
  30.5 8.8 %correlate.1 = bf16[8,128,128]{2,1,0:T(8,128)(2,1)} custom-call(bf16[32,4,16,128]{3,2,1,0:T(8,128)(2,1)} %all_to_all.25.in_ref, bf16[512,1024]{1,0:T(8,128)(2,1)} %constant.14.clone.long_hi, bf16[512,1024]{1,0:T(8,128)(2,1)} %constant.15.clone.long_lo, f32[512,256]{1,0:T(8,128)} %constant.16.clone.twiddle, bf16[256,256]{1,0:T(8,128)(2,1)} %constant.17.clone.short_hi, ...), custom_call_target="tpu_custom_call" | custom-call | tf_op jit(solution)/shard_map/correlate/pallas_call | solution.py:210
  39.3 6.4 %all-to-all-start.1 = ((bf16[8,128,128]{2,1,0:T(8,128)(2,1)}), bf16[8,128,128]{2,1,0:T(8,128)(2,1)S(1)}, u32[]{:S(2)}, u32[]{:S(2)}) async-start(bf16[8,128,128]{2,1,0:T(8,128)(2,1)} %correlate.1), calls=%async_computation.1 | async-start | bytes 524288 | tf_op jit(solution)/shard_map/all_to_all | solution.py:236
  45.7 1.8 %pack_next.1 = bf16[32,2,16,128]{3,2,1,0:T(8,128)(2,1)} custom-call(bf16[64,2048]{1,0:T(8,128)(2,1)} %bitcast.34), custom_call_target="tpu_custom_call" | custom-call | tf_op jit(solution)/shard_map/pack_next/pallas_call | solution.py:210
  47.5 5.9 %all-to-all-done.1.grad_ref = bf16[8,128,128]{2,1,0:T(8,128)(2,1)S(1)} async-done(((bf16[8,128,128]{2,1,0:T(8,128)(2,1)}), bf16[8,128,128]{2,1,0:T(8,128)(2,1)S(1)}, u32[]{:S(2)}, u32[]{:S(2)}) %all-to-all-start.1) | async-done | bytes 262176 | tf_op jit(solution)/shard_map/all_to_all | solution.py:236
  53.3 0.0 copy-start.2
  53.3 0.7 copy-done.2
  54.0 7.0 %all-to-all-start.3 = ((bf16[32,2,16,128]{3,2,1,0:T(8,128)(2,1)}), bf16[32,2,16,128]{3,2,1,0:T(8,128)(2,1)S(1)}, u32[]{:S(2)}, u32[]{:S(2)}) async-start(bf16[32,2,16,128]{3,2,1,0:T(8,128)(2,1)} %pack_next.1), calls=%async_computation.3 | async-start | bytes 524288 | tf_op jit(solution)/shard_map/all_to_all | solution.py:236
  61.0 1.8 %adam.1 = (f32[128,128]{1,0:T(8,128)}, f32[128,128]{1,0:T(8,128)}, f32[128,128]{1,0:T(8,128)}, bf16[8,128,128]{2,1,0:T(8,128)(2,1)}) custom-call(bf16[8,128,128]{2,1,0:T(8,128)(2,1)} %copy-done.2, f32[128,128]{1,0:T(8,128)} %bitcast.38, f32[128,128]{1,0:T(8,128)} %bitcast.39, f32[128,128]{1,0:T(8,128)} %bitcast.40), custom_call_target="tpu_custom_call" | custom-call | tf_op jit(solution)/shard_map/adam/pallas_call | solution.py:210
  62.9 10.1 %all-to-all-done.3.in_ref = bf16[32,2,16,128]{3,2,1,0:T(8,128)(2,1)S(1)} async-done(((bf16[32,2,16,128]{3,2,1,0:T(8,128)(2,1)}), bf16[32,2,16,128]{3,2,1,0:T(8,128)(2,1)S(1)}, u32[]{:S(2)}, u32[]{:S(2)}) %all-to-all-start.3) | async-done | bytes 262176 | tf_op jit(solution)/shard_map/all_to_all | solution.py:236
  72.9 0.0 copy-start
  72.9 0.7 copy-done
  73.6 3.4 %all-to-all-start.2 = ((bf16[8,128,128]{2,1,0:T(8,128)(2,1)}), bf16[8,128,128]{2,1,0:T(8,128)(2,1)S(1)}, u32[]{:S(2)}, u32[]{:S(2)}) async-start(bf16[8,128,128]{2,1,0:T(8,128)(2,1)} %get-tuple-element.11), calls=%async_computation.2 | async-start | bytes 524288 | tf_op jit(solution)/shard_map/all_to_all | solution.py:236
  77.0 5.6 %spectrum.1.next_ref = f32[2,512,256]{2,1,0:T(8,128)} custom-call(bf16[32,2,16,128]{3,2,1,0:T(8,128)(2,1)} %copy-done, bf16[512,1024]{1,0:T(8,128)(2,1)} %constant.14.clone.long_hi, bf16[512,1024]{1,0:T(8,128)(2,1)} %constant.15.clone.long_lo, f32[512,256]{1,0:T(8,128)} %constant.16.clone.twiddle, bf16[256,256]{1,0:T(8,128)(2,1)} %constant.17.clone.short_hi, ...), custom_call_target="tpu_custom_call" | custom-call | tf_op jit(solution)/shard_map/spectrum/pallas_call | solution.py:210
  82.6 2.0 %all-to-all-done.2.in_ref = bf16[8,128,128]{2,1,0:T(8,128)(2,1)S(1)} async-done(((bf16[8,128,128]{2,1,0:T(8,128)(2,1)}), bf16[8,128,128]{2,1,0:T(8,128)(2,1)S(1)}, u32[]{:S(2)}, u32[]{:S(2)}) %all-to-all-start.2) | async-done | bytes 262176 | tf_op jit(solution)/shard_map/all_to_all | solution.py:236
  84.6 0.0 copy-start.1
  84.6 0.7 copy-done.1
  85.3 7.7 %convolve.1 = bf16[32,2,16,128]{3,2,1,0:T(8,128)(2,1)} custom-call(bf16[8,128,128]{2,1,0:T(8,128)(2,1)} %copy-done.1, f32[2,512,256]{2,1,0:T(8,128)} %spectrum.1.next_ref, bf16[512,1024]{1,0:T(8,128)(2,1)} %constant.14.clone.long_hi, bf16[512,1024]{1,0:T(8,128)(2,1)} %constant.15.clone.long_lo, f32[512,256]{1,0:T(8,128)} %constant.16.clone.twiddle, ...), custom_call_target="tpu_custom_call" | custom-call | tf_op jit(solution)/shard_map/convolve/pallas_call | solution.py:210
  93.1 18.9 %all_to_all.26.in_ref = bf16[32,2,16,128]{3,2,1,0:T(8,128)(2,1)} all-to-all(bf16[32,2,16,128]{3,2,1,0:T(8,128)(2,1)} %convolve.1), channel_id=1, replica_groups=mesh['dp'=8,'ctx'=32] {'ctx'}, dimensions={0} | all-to-all | bytes 524288 | tf_op jit(solution)/shard_map/all_to_all | solution.py:236
  111.9 1.9 %unpack.1 = bf16[64,2048]{1,0:T(8,128)(2,1)} custom-call(bf16[32,2,16,128]{3,2,1,0:T(8,128)(2,1)} %all_to_all.26.in_ref), custom_call_target="tpu_custom_call" | custom-call | tf_op jit(solution)/shard_map/unpack/pallas_call | solution.py:210
Async XLA Ops:
  39.3 14.0 %all-to-all-start.1 = ((bf16[8,128,128]{2,1,0:T(8,128)(2,1)}), bf16[8,128,128]{2,1,0:T(8,128)(2,1)S(1)}, u32[]{:S(2)}, u32[]{:S(2)}) async-start(bf16[8,128,128]{2,1,0:T(8,128)(2,1)} %correlate.1), calls=%async_computation.1 | async-start | bytes 524288 | tf_op jit(solution)/shard_map/all_to_all | solution.py:236
  53.3 0.7 copy-start.2
  54.0 18.9 %all-to-all-start.3 = ((bf16[32,2,16,128]{3,2,1,0:T(8,128)(2,1)}), bf16[32,2,16,128]{3,2,1,0:T(8,128)(2,1)S(1)}, u32[]{:S(2)}, u32[]{:S(2)}) async-start(bf16[32,2,16,128]{3,2,1,0:T(8,128)(2,1)} %pack_next.1), calls=%async_computation.3 | async-start | bytes 524288 | tf_op jit(solution)/shard_map/all_to_all | solution.py:236
  72.9 0.7 copy-start
  73.6 11.0 %all-to-all-start.2 = ((bf16[8,128,128]{2,1,0:T(8,128)(2,1)}), bf16[8,128,128]{2,1,0:T(8,128)(2,1)S(1)}, u32[]{:S(2)}, u32[]{:S(2)}) async-start(bf16[8,128,128]{2,1,0:T(8,128)(2,1)} %get-tuple-element.11), calls=%async_computation.2 | async-start | bytes 524288 | tf_op jit(solution)/shard_map/all_to_all | solution.py:236
  84.6 0.7 copy-start.1

commit v2 on v1

--- a/solution.py
+++ b/solution.py
@@ -99,16 +99,28 @@
     return jnp.concatenate(parts, axis=1)
 
 
+def fetch(sources, places, semaphores):
+    copies = [
+        pltpu.make_async_copy(source, place, semaphores.at[i])
+        for i, (source, place) in enumerate(zip(sources, places))
+    ]
+    for copy in copies:
+        copy.start()
+    return copies
+
+
 def pack_body(*refs):
-    count = len(refs) // 2 - 1 + len(refs) % 2
-    sources, out_ref, scratch = refs[:count], refs[count], refs[count + 1 :]
-    for i, ref in enumerate(sources):
-        values = ref[...].astype(f32)
-        channels, length = values.shape
-        pieces = length // LANES
+    count = (len(refs) - 2) // 3
+    sources, out_ref, semaphores = refs[:count], refs[count], refs[-1]
+    arrived, scratch = refs[count + 1 : 2 * count + 1], refs[2 * count + 1 : -1]
+    copies = fetch(sources, arrived, semaphores)
+    peers, _, pieces, _ = out_ref.shape
+    for i in range(count):
+        copies[i].wait()
+        channels = arrived[i].shape[0]
         for k in range(pieces):
-            scratch[i][pl.ds(k, channels, stride=pieces), :] = values[:, k * LANES : (k + 1) * LANES]
-        peers = out_ref.shape[0]
+            lanes = slice(k * LANES, (k + 1) * LANES)
+            scratch[i][pl.ds(k, channels, stride=pieces), :] = arrived[i][:, lanes].astype(f32)
         out_ref[:, 2 * i : 2 * i + 2] = scratch[i][...].reshape(peers, 2, pieces, LANES).astype(bf16)
 
 
@@ -145,45 +157,56 @@
     out_ref[...] = scratch[...].astype(bf16).reshape(out_ref.shape)
 
 
-def adam_body(grad_ref, master, one, two, new_master, new_one, new_two, filters):
+def adam_body(grad_ref, master, one, two, new_master, new_one, new_two, filters, rounded, semaphores):
     grad = grad_ref[0].astype(f32)
     for q in range(1, grad_ref.shape[0]):
         grad = grad + grad_ref[q].astype(f32)
     first = 0.9 * one[...] + 0.1 * grad
     second = 0.999 * two[...] + 0.001 * grad * grad
-    new_one[...] = first
-    new_two[...] = second
     first_hat = first / (1.0 - 0.9**10)
     second_hat = second / (1.0 - 0.999**10)
     old = master[...]
     new = old - 0.01 * (first_hat / (jnp.sqrt(second_hat) + 1e-08) + 0.1 * old)
+    rounded[...] = new.astype(bf16)
+    owners = filters.shape[0]
+    copies = fetch([rounded] * owners, [filters.at[q] for q in range(owners)], semaphores)
+    new_one[...] = first
+    new_two[...] = second
     new_master[...] = new
-    rounded = new.astype(bf16)
-    for q in range(filters.shape[0]):
-        filters[q] = rounded
-
-
-def spectrum_body(in_ref, long_hi, long_lo, twiddle, short_hi, short_lo, out_ref):
-    wave = wave_of(in_ref, 0)
-
-    def step(b, carry):
-        start = pl.multiple_of(b * BLOCK, BLOCK)
+    for copy in copies:
+        copy.wait()
+
+
+def spectrum_body(in_ref, long_hi, long_lo, twiddle, short_hi, short_lo, out_ref, result, semaphores):
+    wave = wave_of(in_ref, 4)
+    copies = []
+    for b in range(ROWS // BLOCK):
+        start = b * BLOCK
+        rows = pl.ds(start, BLOCK)
         spectra = forward_block(start, (wave,), long_hi, long_lo, twiddle, short_hi, short_lo)
         for c in range(2):
-            out_ref[c, pl.ds(start, BLOCK), :] = spectra[c]
-        return carry
-
-    lax.fori_loop(0, ROWS // BLOCK, step, 0)
+            result[c, rows, :] = spectra[c]
+        copies += fetch([result.at[:, rows, :]], [out_ref.at[:, rows, :]], semaphores.at[pl.ds(b, 1)])
+    for copy in copies:
+        copy.wait()
 
 
 def convolve_body(
-    in_ref, next_ref, long_hi, long_lo, twiddle, short_hi, short_lo, back_hi, back_lo,
-    out_ref, high_ref, low_ref, scratch,
+    long_hi, long_lo, in_hbm, next_hbm, twiddle_hbm, short_hi_hbm, short_lo_hbm, back_hi_hbm, back_lo_hbm,
+    out_ref, high_ref, low_ref, scratch, in_ref, next_ref, twiddle, short_hi, short_lo, back_hi, back_lo, semaphores,
 ):
+    copies = fetch(
+        (in_hbm, twiddle_hbm, short_hi_hbm, short_lo_hbm, next_hbm, back_hi_hbm, back_lo_hbm),
+        (in_ref, twiddle, short_hi, short_lo, next_ref, back_hi, back_lo),
+        semaphores,
+    )
+    copies[0].wait()
     scratch[...] = in_ref[...].reshape(2 * ROWS, LANES).astype(f32)
     wave = jnp.concatenate(
         [scratch[pl.ds(c, ROWS, stride=2), :].astype(bf16) for c in range(2)], axis=1
     )
+    for copy in copies[1:]:
+        copy.wait()
 
     def step(b, carry):
         start = pl.multiple_of(b * BLOCK, BLOCK)
@@ -206,15 +229,23 @@
         out_ref[:, c] = result[:, c * LANES : (c + 1) * LANES].reshape(peers, pieces, LANES)
 
 
-def call(body, name, out_shape, scratch, *args):
+def call(body, name, out_shape, scratch, *args, far=(), far_out=False):
+    near = [pltpu.with_memory_space_constraint(a, pltpu.VMEM) for a in args]
+    far = [pltpu.with_memory_space_constraint(a, pltpu.HBM) for a in far]
+    inside, outside = pl.BlockSpec(memory_space=pltpu.VMEM), pl.BlockSpec(memory_space=pltpu.HBM)
+    out_specs = [inside] * len(out_shape)
+    if far_out:
+        out_specs[-1] = outside
+        out_shape = (*out_shape[:-1], pltpu.HBM(out_shape[-1].shape, out_shape[-1].dtype))
     return pl.pallas_call(
         body,
         out_shape=out_shape,
-        in_specs=[pl.BlockSpec(memory_space=pltpu.VMEM)] * len(args),
-        out_specs=jax.tree.map(lambda _: pl.BlockSpec(memory_space=pltpu.VMEM), out_shape),
+        in_specs=[inside] * len(near) + [outside] * len(far),
+        out_specs=tuple(out_specs),
         scratch_shapes=scratch,
         name=name,
-    )(*args)
+        compiler_params=pltpu.CompilerParams(vmem_limit_bytes=16 << 20),
+    )(*near, *far)
 
 
 def shape(dims, dtype):
@@ -246,33 +277,36 @@
     ahead = (long_hi, long_lo, twiddle, short_hi, short_lo)
     work = [pltpu.VMEM((2 * ROWS, 2 * LANES), bf16)] * 2 + [pltpu.VMEM((2 * ROWS, LANES), f32)]
 
-    packed = call(
-        pack_body, "pack", shape((peers, 4, pieces, LANES), bf16), [pltpu.VMEM((rows, LANES), f32)] * 2,
-        inputs[0], out_grad[0],
-    )
-    next_packed = call(
-        pack_body, "pack_next", shape((peers, 2, pieces, LANES), bf16), [pltpu.VMEM((rows, LANES), f32)],
-        next_inputs[0],
-    )
-    partial = call(
-        correlate_body, "correlate", shape((owners, 2 * ROWS // owners, LANES), bf16), work,
-        exchange(packed, "ctx"), *ahead, back_hi, back_lo,
-    )
-    partials = exchange(partial, "dp")
-    own = shape((2 * ROWS // owners, LANES), f32)
+    sources = (inputs[0], out_grad[0], next_inputs[0])
+    (packed,) = call(
+        pack_body, "pack", (shape((peers, 6, pieces, LANES), bf16),),
+        [pltpu.VMEM((channels, length), bf16)] * 3 + [pltpu.VMEM((rows, LANES), f32)] * 3
+        + [pltpu.SemaphoreType.DMA((3,))],
+        far=sources,
+    )
+    waves = exchange(packed, "ctx")
+    own = (2 * ROWS // owners, LANES)
+    (partial,) = call(
+        correlate_body, "correlate", (shape((owners, *own), bf16),), work, waves, *ahead, back_hi, back_lo
+    )
     new_master, new_one, new_two, filters = call(
-        adam_body, "adam", (own, own, own, shape(partial.shape, bf16)), [],
-        partials, interleave(master), interleave(moment_one), interleave(moment_two),
-    )
-    next_spectrum = call(
-        spectrum_body, "spectrum", shape((2, ROWS, 2 * LANES), f32), [], exchange(next_packed, "ctx"), *ahead
-    )
-    result = call(
-        convolve_body, "convolve", shape((peers, 2, pieces, LANES), bf16), work,
-        exchange(filters, "dp"), next_spectrum, *ahead, back_hi, back_lo,
-    )
-    next_out = call(
-        unpack_body, "unpack", shape((channels, length), bf16), [pltpu.VMEM((rows, LANES), f32)],
+        adam_body, "adam", (shape(own, f32),) * 3 + (shape((owners, *own), bf16),),
+        [pltpu.VMEM(own, bf16), pltpu.SemaphoreType.DMA((owners,))],
+        exchange(partial, "dp"), interleave(master), interleave(moment_one), interleave(moment_two), far_out=True,
+    )
+    spectra = (2, ROWS, 2 * LANES)
+    (next_spectrum,) = call(
+        spectrum_body, "spectrum", (shape(spectra, f32),),
+        [pltpu.VMEM(spectra, f32), pltpu.SemaphoreType.DMA((ROWS // BLOCK,))], waves, *ahead, far_out=True,
+    )
+    far = (exchange(filters, "dp"), next_spectrum, twiddle, short_hi, short_lo, back_hi, back_lo)
+    (result,) = call(
+        convolve_body, "convolve", (shape((peers, 2, pieces, LANES), bf16),),
+        work + [pltpu.VMEM(t.shape, t.dtype) for t in far] + [pltpu.SemaphoreType.DMA((len(far),))],
+        long_hi, long_lo, far=far,
+    )
+    (next_out,) = call(
+        unpack_body, "unpack", (shape((channels, length), bf16),), [pltpu.VMEM((rows, LANES), f32)],
         exchange(result, "ctx"),
     )
     return (deinterleave(new_master, 2), deinterleave(new_one, 2), deinterleave(new_two, 2), next_out[None])

time: 114 us -> 95.4 us (0.84)
  blocking collectives: 46.6 us -> 65.6 us
  waiting for transfers between devices: 17.9 us -> 3.59 us
  starting transfers between devices: 16.7 us -> 4.06 us
  Pallas kernels: 29.8 us -> 20 us
    all_to_all x2 -> x3, blocking collectives: 46.6 us -> 65.6 us  [exchange(): return lax.all_to_all(values, axis, split_axis=0, concat_axis=0, tiled=True)]
    all_to_all x3 -> x1, waiting for transfers between devices: 17.9 us -> 3.59 us  [exchange(): return lax.all_to_all(values, axis, split_axis=0, concat_axis=0, tiled=True)]
    all_to_all x3 -> x1, starting transfers between devices: 16.7 us -> 4.06 us  [exchange(): return lax.all_to_all(values, axis, split_axis=0, concat_axis=0, tiled=True)]
    pallas_call x7 -> x6, Pallas kernels: 29.8 us -> 20 us  [call(): pl.pallas_call(body, out_shape=out_shape, in_specs=[inside] * len(near) +...]
  transfers between devices with their start and end apart: 3 -> 1, of which waited for: 3 -> 1; matrix products, arithmetic and copies ran while one was open for 0% -> 0% of each run, Pallas kernels for 8% -> 3%
where the time goes in v2:
time: 95.4 us; the launch traced here: 95 us
  blocking collectives  65.6 us (69%)
  Pallas kernels  20 us (21%)
  starting transfers between devices  4.06 us (4%)
  waiting for transfers between devices  3.59 us (4%)
  local copies, waits for them, and re-layouts  0.97 us (1%)
    all_to_all x3, blocking collectives, exchange(): return lax.all_to_all(values, axis, split_axis=0, concat_axis=0, tiled=True)  65.6 us
    pallas_call x6, Pallas kernels, call(): pl.pallas_call(body, out_shape=out_shape, in_specs=[inside] * len(near) +...  20 us
    all_to_all x1, starting transfers between devices, exchange(): return lax.all_to_all(values, axis, split_axis=0, concat_axis=0, tiled=True)  4.06 us
    all_to_all x1, waiting for transfers between devices, exchange(): return lax.all_to_all(values, axis, split_axis=0, concat_axis=0, tiled=True)  3.59 us
  transfers between devices with their start and end apart: 1, of which 1 were waited for; matrix products, arithmetic and copies ran while one was open for 0% of the time, Pallas kernels for 3%

profile of v2, /device:TPU:1, one launch (start us, length us, event | category | flops | bytes accessed | tf_op | source)
XLA Modules:
  0.0 95.0 jit_solution(15434581376500361928)
XLA Ops:
  0.6 0.0 copy-start.1
  0.6 0.0 copy-start.3
  0.7 0.0 copy-start.4
  0.7 0.0 copy-start.6
  0.7 0.0 copy-start.7
  0.7 1.9 %pack.1 = bf16[32,6,16,128]{3,2,1,0:T(8,128)(2,1)S(1)} custom-call(bf16[64,2048]{1,0:T(8,128)(2,1)} %bitcast.38, bf16[64,2048]{1,0:T(8,128)(2,1)} %bitcast.39, bf16[64,2048]{1,0:T(8,128)(2,1)} %bitcast.40), custom_call_target="tpu_custom_call" | custom-call | tf_op jit(solution)/shard_map/pack/pallas_call | solution.py:240
  2.6 0.0 copy-start
  2.6 0.0 copy-start.2
  2.6 32.2 %all_to_all.20.in_ref = bf16[32,6,16,128]{3,2,1,0:T(8,128)(2,1)S(1)} all-to-all(bf16[32,6,16,128]{3,2,1,0:T(8,128)(2,1)S(1)} %pack.1), channel_id=1, replica_groups=mesh['dp'=8,'ctx'=32] {'ctx'}, dimensions={0} | all-to-all | bytes 1572864 | tf_op jit(solution)/shard_map/all_to_all | solution.py:267
  34.9 0.0 copy-done.1
  34.9 0.0 copy-done.3
  34.9 0.0 copy-done.4
  34.9 0.0 copy-done.6
  34.9 0.0 copy-done.7
  34.9 0.0 copy-done
  34.9 0.0 copy-done.2
  34.9 6.1 %correlate.1 = bf16[8,128,128]{2,1,0:T(8,128)(2,1)S(1)} custom-call(bf16[32,6,16,128]{3,2,1,0:T(8,128)(2,1)S(1)} %all_to_all.20.in_ref, bf16[512,1024]{1,0:T(8,128)(2,1)S(1)} %copy-done.1, bf16[512,1024]{1,0:T(8,128)(2,1)S(1)} %copy-done, f32[512,256]{1,0:T(8,128)S(1)} %copy-done.2, bf16[256,256]{1,0:T(8,128)(2,1)S(1)} %copy-done.4, ...), custom_call_target="tpu_custom_call" | custom-call | tf_op jit(solution)/shard_map/correlate/pallas_call | solution.py:240
  41.0 0.0 copy-start.8
  41.1 0.0 copy-start.9
  41.1 0.0 copy-start.10
  41.1 14.0 %all_to_all.21.grad_ref = bf16[8,128,128]{2,1,0:T(8,128)(2,1)S(1)} all-to-all(bf16[8,128,128]{2,1,0:T(8,128)(2,1)S(1)} %correlate.1), channel_id=1, replica_groups=mesh['dp'=8,'ctx'=32] {'dp'}, dimensions={0} | all-to-all | bytes 524288 | tf_op jit(solution)/shard_map/all_to_all | solution.py:267
  55.0 0.0 copy-done.8
  55.0 0.0 copy-done.9
  55.0 0.0 copy-done.10
  55.1 1.5 %adam.1 = (f32[128,128]{1,0:T(8,128)}, f32[128,128]{1,0:T(8,128)}, f32[128,128]{1,0:T(8,128)}, bf16[8,128,128]{2,1,0:T(8,128)(2,1)}) custom-call(bf16[8,128,128]{2,1,0:T(8,128)(2,1)S(1)} %all_to_all.21.grad_ref, f32[128,128]{1,0:T(8,128)S(1)} %bitcast.34, f32[128,128]{1,0:T(8,128)S(1)} %bitcast.35, f32[128,128]{1,0:T(8,128)S(1)} %bitcast.36), custom_call_target="tpu_custom_call" | custom-call | tf_op jit(solution)/shard_map/adam/pallas_call | solution.py:240
  56.6 4.1 %all-to-all-start.2 = ((bf16[8,128,128]{2,1,0:T(8,128)(2,1)}), bf16[8,128,128]{2,1,0:T(8,128)(2,1)}, u32[]{:S(2)}, u32[]{:S(2)}) async-start(bf16[8,128,128]{2,1,0:T(8,128)(2,1)} %get-tuple-element.11), calls=%async_computation.2 | async-start | bytes 524288 | tf_op jit(solution)/shard_map/all_to_all | solution.py:267
  60.7 0.0 copy-start.5
  60.7 0.9 copy-done.5
  61.6 3.1 %spectrum.1.next_hbm = f32[2,512,256]{2,1,0:T(8,128)} custom-call(bf16[32,6,16,128]{3,2,1,0:T(8,128)(2,1)S(1)} %all_to_all.20.in_ref, bf16[512,1024]{1,0:T(8,128)(2,1)S(1)} %copy-done.1, bf16[512,1024]{1,0:T(8,128)(2,1)S(1)} %copy-done, f32[512,256]{1,0:T(8,128)S(1)} %copy-done.2, bf16[256,256]{1,0:T(8,128)(2,1)S(1)} %copy-done.5, bf16[256,256]{1,0:T(8,128)(2,1)S(1)} %copy-done.3), custom_call_target="tpu_custom_call" | custom-call | tf_op jit(solution)/shard_map/spectrum/pallas_call | solution.py:240
  64.7 3.6 %all-to-all-done.2.in_hbm = bf16[8,128,128]{2,1,0:T(8,128)(2,1)} async-done(((bf16[8,128,128]{2,1,0:T(8,128)(2,1)}), bf16[8,128,128]{2,1,0:T(8,128)(2,1)}, u32[]{:S(2)}, u32[]{:S(2)}) %all-to-all-start.2) | async-done | bytes 262176 | tf_op jit(solution)/shard_map/all_to_all | solution.py:267
  68.3 6.4 %convolve.1 = bf16[32,2,16,128]{3,2,1,0:T(8,128)(2,1)S(1)} custom-call(bf16[512,1024]{1,0:T(8,128)(2,1)S(1)} %copy-done.1, bf16[512,1024]{1,0:T(8,128)(2,1)S(1)} %copy-done, bf16[8,128,128]{2,1,0:T(8,128)(2,1)} %all-to-all-done.2.in_hbm, f32[2,512,256]{2,1,0:T(8,128)} %spectrum.1.next_hbm, f32[512,256]{1,0:T(8,128)} %constant.16.clone.twiddle.twiddle_hbm, ...), custom_call_target="tpu_custom_call" | custom-call | tf_op jit(solution)/shard_map/convolve/pallas_call | solution.py:240
  74.7 19.4 %all_to_all.22.in_ref = bf16[32,2,16,128]{3,2,1,0:T(8,128)(2,1)S(1)} all-to-all(bf16[32,2,16,128]{3,2,1,0:T(8,128)(2,1)S(1)} %convolve.1), channel_id=1, replica_groups=mesh['dp'=8,'ctx'=32] {'ctx'}, dimensions={0} | all-to-all | bytes 524288 | tf_op jit(solution)/shard_map/all_to_all | solution.py:267
  94.1 0.9 unpack.1
Async XLA Ops:
  0.6 34.3 %copy-start.1 = (bf16[512,1024]{1,0:T(8,128)(2,1)S(1)}, bf16[512,1024]{1,0:T(8,128)(2,1)}, u32[]{:S(2)}) copy-start(bf16[512,1024]{1,0:T(8,128)(2,1)} %constant.14.clone.long_hi) | copy-start | bytes 3145732
  0.6 34.2 %copy-start.3 = (bf16[256,256]{1,0:T(8,128)(2,1)S(1)}, bf16[256,256]{1,0:T(8,128)(2,1)}, u32[]{:S(2)}) copy-start(bf16[256,256]{1,0:T(8,128)(2,1)} %constant.18.clone.short_lo.short_lo_hbm) | copy-start | bytes 393220
  0.7 34.2 %copy-start.4 = (bf16[256,256]{1,0:T(8,128)(2,1)S(1)}, bf16[256,256]{1,0:T(8,128)(2,1)}, u32[]{:S(2)}) copy-start(bf16[256,256]{1,0:T(8,128)(2,1)} %constant.17.clone.short_hi.short_hi_hbm) | copy-start | bytes 393220
  0.7 34.2 %copy-start.6 = (bf16[256,256]{1,0:T(8,128)(2,1)S(1)}, bf16[256,256]{1,0:T(8,128)(2,1)}, u32[]{:S(2)}) copy-start(bf16[256,256]{1,0:T(8,128)(2,1)} %constant.20.clone.back_lo.back_lo_hbm) | copy-start | bytes 393220
  0.7 34.2 %copy-start.7 = (bf16[256,256]{1,0:T(8,128)(2,1)S(1)}, bf16[256,256]{1,0:T(8,128)(2,1)}, u32[]{:S(2)}) copy-start(bf16[256,256]{1,0:T(8,128)(2,1)} %constant.19.clone.back_hi.back_hi_hbm) | copy-start | bytes 393220
  2.6 32.3 %copy-start = (bf16[512,1024]{1,0:T(8,128)(2,1)S(1)}, bf16[512,1024]{1,0:T(8,128)(2,1)}, u32[]{:S(2)}) copy-start(bf16[512,1024]{1,0:T(8,128)(2,1)} %constant.15.clone.long_lo) | copy-start | bytes 3145732
  2.6 32.3 %copy-start.2 = (f32[512,256]{1,0:T(8,128)S(1)}, f32[512,256]{1,0:T(8,128)}, u32[]{:S(2)}) copy-start(f32[512,256]{1,0:T(8,128)} %constant.16.clone.twiddle.twiddle_hbm) | copy-start | bytes 1572868
  41.0 14.0 %copy-start.8 = (f32[2,8192]{1,0:T(2,128)S(1)}, f32[2,8192]{1,0:T(2,128)}, u32[]{:S(2)}) copy-start(f32[2,8192]{1,0:T(2,128)} %param.15) | copy-start | bytes 196612
  41.1 14.0 %copy-start.9 = (f32[2,8192]{1,0:T(2,128)S(1)}, f32[2,8192]{1,0:T(2,128)}, u32[]{:S(2)}) copy-start(f32[2,8192]{1,0:T(2,128)} %param.16) | copy-start | bytes 196612
  41.1 14.0 %copy-start.10 = (f32[2,8192]{1,0:T(2,128)S(1)}, f32[2,8192]{1,0:T(2,128)}, u32[]{:S(2)}) copy-start(f32[2,8192]{1,0:T(2,128)} %param.17) | copy-start | bytes 196612
  56.6 11.7 %all-to-all-start.2 = ((bf16[8,128,128]{2,1,0:T(8,128)(2,1)}), bf16[8,128,128]{2,1,0:T(8,128)(2,1)}, u32[]{:S(2)}, u32[]{:S(2)}) async-start(bf16[8,128,128]{2,1,0:T(8,128)(2,1)} %get-tuple-element.11), calls=%async_computation.2 | async-start | bytes 524288 | tf_op jit(solution)/shard_map/all_to_all | solution.py:267
  60.7 0.9 copy-start.5

commit v3 on v2

v3 whole, which is shorter than its diff:
```python
import math

import jax
import jax.numpy as jnp
import numpy as np
from jax import lax
from jax.experimental import pallas as pl
from jax.experimental.pallas import tpu as pltpu
from jax.sharding import PartitionSpec as P

ROWS = 512
LANES = 128
BLOCK = 128

f32 = jnp.float32
bf16 = jnp.bfloat16


def split_table(values):
    high = values.astype(bf16)
    low = (values - high.astype(np.float64)).astype(bf16)
    return high, low


def tables():
    half = np.arange(ROWS) + 0.5
    lanes = np.arange(LANES)
    outer = 2.0 * math.pi * np.outer(half, half) / (2 * ROWS)
    long_hi, long_lo = split_table(np.concatenate([np.cos(outer), np.sin(outer)], axis=0))
    turn = 2.0 * math.pi * np.outer(half, lanes / (2.0 * ROWS * LANES) - 1.0 / (4 * ROWS))
    twiddle = np.concatenate([np.cos(turn), np.sin(turn)], axis=1).astype(np.float32)
    inner = 2.0 * math.pi * (np.outer(lanes, lanes) % LANES) / LANES
    cosine, sine = np.cos(inner), np.sin(inner)
    short = np.block([[cosine, sine], [-sine, cosine]])
    short_hi, short_lo = split_table(short)
    fore, rear = slice(0, ROWS // 2), slice(ROWS // 2, ROWS)
    double = lambda part: (2.0 * part.astype(np.float64)).astype(bf16)
    long = np.concatenate(
        [long_hi[:, fore], long_lo[:, fore], double(long_hi[:, rear]), double(long_lo[:, rear])], axis=1
    )
    return (long, twiddle, short_hi, short_lo)


def dot(left, right):
    return jnp.dot(left, right, preferred_element_type=f32)


def store_halves(values, place, high_ref, low_ref):
    high = values.astype(bf16)
    high_ref[place] = high
    low_ref[place] = (values - high.astype(f32)).astype(bf16)


def times_short(high_ref, low_ref, rows, hi_ref, lo_ref):
    left = jnp.concatenate([high_ref[rows], low_ref[rows], high_ref[rows]], axis=1)
    right = jnp.concatenate([hi_ref[...], hi_ref[...], lo_ref[...]], axis=0)
    return dot(left, right)


def channel_rows(c):
    return slice(c * ROWS, (c + 1) * ROWS)


def channel_lanes(c):
    return slice(c * LANES, (c + 1) * LANES)


def forward(waves, long, twiddle, short_hi, short_lo, high_ref, low_ref):
    left, right = slice(0, LANES), slice(LANES, 2 * LANES)
    half = ROWS // 2
    spectra = []
    for wave in waves:
        fore = dot(long[:, :ROWS], jnp.concatenate([wave[:half], wave[:half]], axis=0))
        rear = dot(long[:, ROWS:], jnp.concatenate([wave[half:], wave[half:]], axis=0))
        first = fore + 0.5 * rear
        done = len(spectra)
        for c in range(2):
            at = channel_rows(done + c)
            real, imag = first[:ROWS, channel_lanes(c)], first[ROWS:, channel_lanes(c)]
            cosine, sine = twiddle[:, left], twiddle[:, right]
            store_halves(real * cosine - imag * sine, (at, left), high_ref, low_ref)
            store_halves(real * sine + imag * cosine, (at, right), high_ref, low_ref)
        for c in range(2):
            spectra.append(times_short(high_ref, low_ref, channel_rows(done + c), short_hi, short_lo))
    return spectra


def backward(products, long, twiddle, short_hi, short_lo, high_ref, low_ref, wide_hi, wide_lo):
    left, right = slice(0, LANES), slice(LANES, 2 * LANES)
    half = ROWS // 2
    top, end = slice(0, ROWS), slice(ROWS, 2 * ROWS)
    for c, (real, imag) in enumerate(products):
        store_halves(real, (channel_rows(c), left), high_ref, low_ref)
        store_halves(-imag, (channel_rows(c), right), high_ref, low_ref)
    mixed = [
        times_short(high_ref, low_ref, channel_rows(c), short_hi, short_lo) for c in range(len(products))
    ]
    for c in range(len(products)):
        cosine, sine = twiddle[:, left], twiddle[:, right]
        mixed_re, mixed_im = mixed[c][:, left], mixed[c][:, right]
        store_halves(mixed_re * cosine - mixed_im * sine, (top, channel_lanes(c)), wide_hi, wide_lo)
        store_halves(-(mixed_im * cosine + mixed_re * sine), (end, channel_lanes(c)), wide_hi, wide_lo)
    total = []
    for at in (0, half):
        both, high = slice(2 * at, 2 * at + ROWS), slice(2 * at, 2 * at + half)
        real, imag = slice(at, at + half), slice(ROWS + at, ROWS + at + half)
        table = jnp.concatenate([long[top, both], long[end, both], long[top, high], long[end, high]], axis=1)
        waves = [wide_hi[real], wide_hi[real], wide_hi[imag], wide_hi[imag], wide_lo[real], wide_lo[imag]]
        total.append(dot(table, jnp.concatenate(waves, axis=0)))
    scale = 1.0 / (ROWS * LANES)
    return total[0] * scale + total[1] * (0.5 * scale)


def wave_of(ref, first):
    parts = [ref[:, first + c].reshape(ROWS, LANES) for c in range(2)]
    return jnp.concatenate(parts, axis=1)


def fetch(sources, places, semaphores):
    copies = [
        pltpu.make_async_copy(source, place, semaphores.at[i])
        for i, (source, place) in enumerate(zip(sources, places))
    ]
    for copy in copies:
        copy.start()
    return copies


def pack_body(*refs):
    count = (len(refs) - 2) // 3
    sources, out_ref, semaphores = refs[:count], refs[count], refs[-1]
    arrived, scratch = refs[count + 1 : 2 * count + 1], refs[2 * count + 1 : -1]
    copies = fetch(sources, arrived, semaphores)
    peers, _, pieces, _ = out_ref.shape
    for i in range(count):
        copies[i].wait()
        channels = arrived[i].shape[0]
        for k in range(pieces):
            lanes = slice(k * LANES, (k + 1) * LANES)
            scratch[i][pl.ds(k, channels, stride=pieces), :] = arrived[i][:, lanes].astype(f32)
        out_ref[:, 2 * i : 2 * i + 2] = scratch[i][...].reshape(peers, 2, pieces, LANES).astype(bf16)


def unpack_body(in_ref, out_ref, scratch):
    channels, length = out_ref.shape
    pieces = length // LANES
    scratch[...] = in_ref[...].astype(f32).reshape(channels * pieces, LANES)
    for k in range(pieces):
        out_ref[:, k * LANES : (k + 1) * LANES] = scratch[pl.ds(k, channels, stride=pieces), :].astype(bf16)


def correlate_body(
    in_ref, long, twiddle, short_hi, short_lo, out_ref, high_ref, low_ref, wide_hi, wide_lo, scratch
):
    waves = wave_of(in_ref, 0), wave_of(in_ref, 2)
    spectra = forward(waves, long, twiddle, short_hi, short_lo, high_ref, low_ref)
    products = []
    for c in range(2):
        s_re, s_im = spectra[c][:, :LANES], spectra[c][:, LANES:]
        g_re, g_im = spectra[2 + c][:, :LANES], spectra[2 + c][:, LANES:]
        products.append((g_re * s_re + g_im * s_im, g_im * s_re - g_re * s_im))
    result = backward(products, long, twiddle, short_hi, short_lo, high_ref, low_ref, wide_hi, wide_lo)
    for c in range(2):
        scratch[pl.ds(c, ROWS, stride=2), :] = result[:, channel_lanes(c)]
    out_ref[...] = scratch[...].astype(bf16).reshape(out_ref.shape)


def adam_body(grad_ref, master, one, two, new_master, new_one, new_two, filters, rounded, semaphores):
    grad = grad_ref[0].astype(f32)
    for q in range(1, grad_ref.shape[0]):
        grad = grad + grad_ref[q].astype(f32)
    first = 0.9 * one[...] + 0.1 * grad
    second = 0.999 * two[...] + 0.001 * grad * grad
    first_hat = first / (1.0 - 0.9**10)
    second_hat = second / (1.0 - 0.999**10)
    old = master[...]
    new = old - 0.01 * (first_hat / (jnp.sqrt(second_hat) + 1e-08) + 0.1 * old)
    rounded[...] = new.astype(bf16)
    owners = filters.shape[0]
    copies = fetch([rounded] * owners, [filters.at[q] for q in range(owners)], semaphores)
    new_one[...] = first
    new_two[...] = second
    new_master[...] = new
    for copy in copies:
        copy.wait()


def spectrum_body(in_ref, long, twiddle, short_hi, short_lo, out_ref, high_ref, low_ref, result, semaphores):
    spectra = forward((wave_of(in_ref, 4),), long, twiddle, short_hi, short_lo, high_ref, low_ref)
    for c in range(2):
        result[channel_rows(c), :] = spectra[c]
    for copy in fetch([result], [out_ref], semaphores):
        copy.wait()


def convolve_body(
    long, in_hbm, next_hbm, twiddle_hbm, short_hi_hbm, short_lo_hbm,
    out_ref, high_ref, low_ref, wide_hi, wide_lo, scratch,
    in_ref, next_ref, twiddle, short_hi, short_lo, semaphores,
):
    copies = fetch(
        (in_hbm, twiddle_hbm, short_hi_hbm, short_lo_hbm, next_hbm),
        (in_ref, twiddle, short_hi, short_lo, next_ref),
        semaphores,
    )
    copies[0].wait()
    scratch[...] = in_ref[...].reshape(2 * ROWS, LANES).astype(f32)
    wave = jnp.concatenate(
        [scratch[pl.ds(c, ROWS, stride=2), :].astype(bf16) for c in range(2)], axis=1
    )
    for copy in copies[1:]:
        copy.wait()
    spectra = forward((wave,), long, twiddle, short_hi, short_lo, high_ref, low_ref)
    products = []
    for c in range(2):
        f_re, f_im = spectra[c][:, :LANES], spectra[c][:, LANES:]
        n_re, n_im = next_ref[channel_rows(c), :LANES], next_ref[channel_rows(c), LANES:]
        products.append((f_re * n_re - f_im * n_im, f_re * n_im + f_im * n_re))
    result = backward(products, long, twiddle, short_hi, short_lo, high_ref, low_ref, wide_hi, wide_lo)
    result = result.astype(bf16)
    peers, pieces = out_ref.shape[0], out_ref.shape[2]
    for c in range(2):
        out_ref[:, c] = result[:, channel_lanes(c)].reshape(peers, pieces, LANES)


def call(body, name, out_shape, scratch, *args, far=(), far_out=False):
    near = [pltpu.with_memory_space_constraint(a, pltpu.VMEM) for a in args]
    far = [pltpu.with_memory_space_constraint(a, pltpu.HBM) for a in far]
    inside, outside = pl.BlockSpec(memory_space=pltpu.VMEM), pl.BlockSpec(memory_space=pltpu.HBM)
    out_specs = [inside] * len(out_shape)
    if far_out:
        out_specs[-1] = outside
        out_shape = (*out_shape[:-1], pltpu.HBM(out_shape[-1].shape, out_shape[-1].dtype))
    return pl.pallas_call(
        body,
        out_shape=out_shape,
        in_specs=[inside] * len(near) + [outside] * len(far),
        out_specs=tuple(out_specs),
        scratch_shapes=scratch,
        name=name,
        compiler_params=pltpu.CompilerParams(vmem_limit_bytes=16 << 20),
    )(*near, *far)


def shape(dims, dtype):
    return jax.ShapeDtypeStruct(dims, dtype)


def interleave(values):
    channels, taps = values.shape
    pieces = taps // LANES
    return values.reshape(channels, pieces, LANES).transpose(1, 0, 2).reshape(channels * pieces, LANES)


def deinterleave(values, channels):
    pieces = values.shape[0] // channels
    return values.reshape(pieces, channels, LANES).transpose(1, 0, 2).reshape(channels, pieces * LANES)


def exchange(values, axis):
    return lax.all_to_all(values, axis, split_axis=0, concat_axis=0, tiled=True)


def local(inputs, out_grad, master, moment_one, moment_two, next_inputs):
    channels, length = inputs.shape[1:]
    peers = lax.axis_size("ctx")
    owners = lax.axis_size("dp")
    pieces = length // LANES
    rows = channels * pieces
    long, twiddle, short_hi, short_lo = (jnp.asarray(t) for t in tables())
    ahead = (long, twiddle, short_hi, short_lo)
    wide = [pltpu.VMEM((2 * ROWS, 2 * LANES), bf16)] * 2
    tall = [pltpu.VMEM((4 * ROWS, 2 * LANES), bf16)] * 2
    narrow = [pltpu.VMEM((2 * ROWS, LANES), f32)]

    sources = (inputs[0], out_grad[0], next_inputs[0])
    (packed,) = call(
        pack_body, "pack", (shape((peers, 6, pieces, LANES), bf16),),
        [pltpu.VMEM((channels, length), bf16)] * 3 + [pltpu.VMEM((rows, LANES), f32)] * 3
        + [pltpu.SemaphoreType.DMA((3,))],
        far=sources,
    )
    waves = exchange(packed, "ctx")
    own = (2 * ROWS // owners, LANES)
    (partial,) = call(
        correlate_body, "correlate", (shape((owners, *own), bf16),), tall + wide + narrow, waves, *ahead
    )
    new_master, new_one, new_two, filters = call(
        adam_body, "adam", (shape(own, f32),) * 3 + (shape((owners, *own), bf16),),
        [pltpu.VMEM(own, bf16), pltpu.SemaphoreType.DMA((owners,))],
        exchange(partial, "dp"), interleave(master), interleave(moment_one), interleave(moment_two), far_out=True,
    )
    spectra = (2 * ROWS, 2 * LANES)
    (next_spectrum,) = call(
        spectrum_body, "spectrum", (shape(spectra, f32),),
        wide + [pltpu.VMEM(spectra, f32), pltpu.SemaphoreType.DMA((1,))], waves, *ahead, far_out=True,
    )
    far = (exchange(filters, "dp"), next_spectrum, twiddle, short_hi, short_lo)
    (result,) = call(
        convolve_body, "convolve", (shape((peers, 2, pieces, LANES), bf16),),
        wide + wide + narrow + [pltpu.VMEM(t.shape, t.dtype) for t in far]
        + [pltpu.SemaphoreType.DMA((len(far),))],
        long, far=far,
    )
    (next_out,) = call(
        unpack_body, "unpack", (shape((channels, length), bf16),), [pltpu.VMEM((rows, LANES), f32)],
        exchange(result, "ctx"),
    )
    return (deinterleave(new_master, 2), deinterleave(new_one, 2), deinterleave(new_two, 2), next_out[None])


def solution(mesh):
    return jax.shard_map(
        local,
        mesh=mesh,
        in_specs=(
            P("dp", None, "ctx"),
            P("dp", None, "ctx"),
            P("ctx", "dp"),
            P("ctx", "dp"),
            P("ctx", "dp"),
            P("dp", None, "ctx"),
        ),
        out_specs=(P("ctx", "dp"), P("ctx", "dp"), P("ctx", "dp"), P("dp", None, "ctx")),
        check_vma=False,
    )
```

time: 95.4 us -> 91.5 us (0.959)
  Pallas kernels: 20 us -> 15.7 us
    pallas_call x6, Pallas kernels: 20 us -> 15.7 us  [call(): pl.pallas_call(body, out_shape=out_shape, in_specs=[inside] * len(near) +...]
where the time goes in v3:
time: 91.5 us; the launch traced here: 91.2 us
  blocking collectives  65.4 us (71%)
  Pallas kernels  15.7 us (17%)
  waiting for transfers between devices  4.41 us (5%)
  starting transfers between devices  4.07 us (4%)
  local copies, waits for them, and re-layouts  0.95 us (1%)
    all_to_all x3, blocking collectives, exchange(): return lax.all_to_all(values, axis, split_axis=0, concat_axis=0, tiled=True)  65.4 us
    pallas_call x6, Pallas kernels, call(): pl.pallas_call(body, out_shape=out_shape, in_specs=[inside] * len(near) +...  15.7 us
    all_to_all x1, waiting for transfers between devices, exchange(): return lax.all_to_all(values, axis, split_axis=0, concat_axis=0, tiled=True)  4.41 us
    all_to_all x1, starting transfers between devices, exchange(): return lax.all_to_all(values, axis, split_axis=0, concat_axis=0, tiled=True)  4.07 us
  transfers between devices with their start and end apart: 1, of which 1 were waited for; matrix products, arithmetic and copies ran while one was open for 0% of the time, Pallas kernels for 3%

profile of v3, /device:TPU:1, one launch (start us, length us, event | category | flops | bytes accessed | tf_op | source)
XLA Modules:
  0.0 91.2 jit_solution(982715597745797036)
XLA Ops:
  0.6 0.0 copy-start.2
  0.6 0.0 copy-start.3
  0.7 0.0 copy-start.1
  0.7 0.0 copy-start
  0.7 2.0 %pack.1 = bf16[32,6,16,128]{3,2,1,0:T(8,128)(2,1)S(1)} custom-call(bf16[64,2048]{1,0:T(8,128)(2,1)} %bitcast.38, bf16[64,2048]{1,0:T(8,128)(2,1)} %bitcast.39, bf16[64,2048]{1,0:T(8,128)(2,1)} %bitcast.40), custom_call_target="tpu_custom_call" | custom-call | tf_op jit(solution)/shard_map/pack/pallas_call | solution.py:234
  2.6 32.1 %all_to_all.20.in_ref = bf16[32,6,16,128]{3,2,1,0:T(8,128)(2,1)S(1)} all-to-all(bf16[32,6,16,128]{3,2,1,0:T(8,128)(2,1)S(1)} %pack.1), channel_id=1, replica_groups=mesh['dp'=8,'ctx'=32] {'ctx'}, dimensions={0} | all-to-all | bytes 1572864 | tf_op jit(solution)/shard_map/all_to_all | solution.py:261
  34.8 0.0 copy-done.2
  34.8 0.0 copy-done.3
  34.8 0.0 copy-done.1
  34.8 0.0 copy-done
  34.8 0.0 copy-start.5
  34.8 0.0 copy-start.6
  34.8 0.0 copy-start.7
  34.8 4.3 %correlate.1 = bf16[8,128,128]{2,1,0:T(8,128)(2,1)S(1)} custom-call(bf16[32,6,16,128]{3,2,1,0:T(8,128)(2,1)S(1)} %all_to_all.20.in_ref, bf16[1024,1024]{1,0:T(8,128)(2,1)S(1)} %copy-done, f32[512,256]{1,0:T(8,128)S(1)} %copy-done.1, bf16[256,256]{1,0:T(8,128)(2,1)S(1)} %copy-done.3, bf16[256,256]{1,0:T(8,128)(2,1)S(1)} %copy-done.2), custom_call_target="tpu_custom_call" | custom-call | tf_op jit(solution)/shard_map/correlate/pallas_call | solution.py:234
  39.1 13.8 %all_to_all.21.grad_ref = bf16[8,128,128]{2,1,0:T(8,128)(2,1)S(1)} all-to-all(bf16[8,128,128]{2,1,0:T(8,128)(2,1)S(1)} %correlate.1), channel_id=1, replica_groups=mesh['dp'=8,'ctx'=32] {'dp'}, dimensions={0} | all-to-all | bytes 524288 | tf_op jit(solution)/shard_map/all_to_all | solution.py:261
  52.9 0.0 copy-done.5
  52.9 0.0 copy-done.6
  52.9 0.0 copy-done.7
  53.0 1.5 %adam.1 = (f32[128,128]{1,0:T(8,128)}, f32[128,128]{1,0:T(8,128)}, f32[128,128]{1,0:T(8,128)}, bf16[8,128,128]{2,1,0:T(8,128)(2,1)}) custom-call(bf16[8,128,128]{2,1,0:T(8,128)(2,1)S(1)} %all_to_all.21.grad_ref, f32[128,128]{1,0:T(8,128)S(1)} %bitcast.34, f32[128,128]{1,0:T(8,128)S(1)} %bitcast.35, f32[128,128]{1,0:T(8,128)S(1)} %bitcast.36), custom_call_target="tpu_custom_call" | custom-call | tf_op jit(solution)/shard_map/adam/pallas_call | solution.py:234
  54.5 4.1 %all-to-all-start.2 = ((bf16[8,128,128]{2,1,0:T(8,128)(2,1)}), bf16[8,128,128]{2,1,0:T(8,128)(2,1)}, u32[]{:S(2)}, u32[]{:S(2)}) async-start(bf16[8,128,128]{2,1,0:T(8,128)(2,1)} %get-tuple-element.11), calls=%async_computation.2 | async-start | bytes 524288 | tf_op jit(solution)/shard_map/all_to_all | solution.py:261
  58.6 0.0 copy-start.4
  58.6 0.9 copy-done.4
  59.5 2.3 %spectrum.1.next_hbm = f32[1024,256]{1,0:T(8,128)} custom-call(bf16[32,6,16,128]{3,2,1,0:T(8,128)(2,1)S(1)} %all_to_all.20.in_ref, bf16[1024,1024]{1,0:T(8,128)(2,1)S(1)} %copy-done, f32[512,256]{1,0:T(8,128)S(1)} %copy-done.1, bf16[256,256]{1,0:T(8,128)(2,1)S(1)} %copy-done.4, bf16[256,256]{1,0:T(8,128)(2,1)S(1)} %copy-done.2), custom_call_target="tpu_custom_call" | custom-call | tf_op jit(solution)/shard_map/spectrum/pallas_call | solution.py:234
  61.8 4.4 %all-to-all-done.2.in_hbm = bf16[8,128,128]{2,1,0:T(8,128)(2,1)} async-done(((bf16[8,128,128]{2,1,0:T(8,128)(2,1)}), bf16[8,128,128]{2,1,0:T(8,128)(2,1)}, u32[]{:S(2)}, u32[]{:S(2)}) %all-to-all-start.2) | async-done | bytes 262176 | tf_op jit(solution)/shard_map/all_to_all | solution.py:261
  66.2 4.7 %convolve.1 = bf16[32,2,16,128]{3,2,1,0:T(8,128)(2,1)S(1)} custom-call(bf16[1024,1024]{1,0:T(8,128)(2,1)S(1)} %copy-done, bf16[8,128,128]{2,1,0:T(8,128)(2,1)} %all-to-all-done.2.in_hbm, f32[1024,256]{1,0:T(8,128)} %spectrum.1.next_hbm, f32[512,256]{1,0:T(8,128)} %constant.9.clone.twiddle.twiddle_hbm, bf16[256,256]{1,0:T(8,128)(2,1)} %constant.10.clone.short_hi.short_hi_hbm, ...), custom_call_target="tpu_custom_call" | custom-call | tf_op jit(solution)/shard_map/convolve/pallas_call | solution.py:234
  70.9 19.4 %all_to_all.22.in_ref = bf16[32,2,16,128]{3,2,1,0:T(8,128)(2,1)S(1)} all-to-all(bf16[32,2,16,128]{3,2,1,0:T(8,128)(2,1)S(1)} %convolve.1), channel_id=1, replica_groups=mesh['dp'=8,'ctx'=32] {'ctx'}, dimensions={0} | all-to-all | bytes 524288 | tf_op jit(solution)/shard_map/all_to_all | solution.py:261
  90.3 0.9 unpack.1
Async XLA Ops:
  0.6 34.1 %copy-start.2 = (bf16[256,256]{1,0:T(8,128)(2,1)S(1)}, bf16[256,256]{1,0:T(8,128)(2,1)}, u32[]{:S(2)}) copy-start(bf16[256,256]{1,0:T(8,128)(2,1)} %constant.11.clone.short_lo.short_lo_hbm) | copy-start | bytes 393220
  0.6 34.1 %copy-start.3 = (bf16[256,256]{1,0:T(8,128)(2,1)S(1)}, bf16[256,256]{1,0:T(8,128)(2,1)}, u32[]{:S(2)}) copy-start(bf16[256,256]{1,0:T(8,128)(2,1)} %constant.10.clone.short_hi.short_hi_hbm) | copy-start | bytes 393220
  0.7 34.1 %copy-start.1 = (f32[512,256]{1,0:T(8,128)S(1)}, f32[512,256]{1,0:T(8,128)}, u32[]{:S(2)}) copy-start(f32[512,256]{1,0:T(8,128)} %constant.9.clone.twiddle.twiddle_hbm) | copy-start | bytes 1572868
  0.7 34.1 %copy-start = (bf16[1024,1024]{1,0:T(8,128)(2,1)S(1)}, bf16[1024,1024]{1,0:T(8,128)(2,1)}, u32[]{:S(2)}) copy-start(bf16[1024,1024]{1,0:T(8,128)(2,1)} %constant.8.clone.long) | copy-start | bytes 6291460
  34.8 18.2 %copy-start.5 = (f32[2,8192]{1,0:T(2,128)S(1)}, f32[2,8192]{1,0:T(2,128)}, u32[]{:S(2)}) copy-start(f32[2,8192]{1,0:T(2,128)} %param.12) | copy-start | bytes 196612
  34.8 18.2 %copy-start.6 = (f32[2,8192]{1,0:T(2,128)S(1)}, f32[2,8192]{1,0:T(2,128)}, u32[]{:S(2)}) copy-start(f32[2,8192]{1,0:T(2,128)} %param.13) | copy-start | bytes 196612
  34.8 18.1 %copy-start.7 = (f32[2,8192]{1,0:T(2,128)S(1)}, f32[2,8192]{1,0:T(2,128)}, u32[]{:S(2)}) copy-start(f32[2,8192]{1,0:T(2,128)} %param.14) | copy-start | bytes 196612
  54.5 11.7 %all-to-all-start.2 = ((bf16[8,128,128]{2,1,0:T(8,128)(2,1)}), bf16[8,128,128]{2,1,0:T(8,128)(2,1)}, u32[]{:S(2)}, u32[]{:S(2)}) async-start(bf16[8,128,128]{2,1,0:T(8,128)(2,1)} %get-tuple-element.11), calls=%async_computation.2 | async-start | bytes 524288 | tf_op jit(solution)/shard_map/all_to_all | solution.py:261
  58.6 0.9 copy-start.4

commit v4 on v3

--- a/solution.py
+++ b/solution.py
@@ -34,10 +34,7 @@
     short = np.block([[cosine, sine], [-sine, cosine]])
     short_hi, short_lo = split_table(short)
     fore, rear = slice(0, ROWS // 2), slice(ROWS // 2, ROWS)
-    double = lambda part: (2.0 * part.astype(np.float64)).astype(bf16)
-    long = np.concatenate(
-        [long_hi[:, fore], long_lo[:, fore], double(long_hi[:, rear]), double(long_lo[:, rear])], axis=1
-    )
+    long = np.concatenate([long_hi[:, fore], long_lo[:, fore], -long_hi[:, rear], -long_lo[:, rear]], axis=1)
     return (long, twiddle, short_hi, short_lo)
 
 
@@ -65,14 +62,14 @@
     return slice(c * LANES, (c + 1) * LANES)
 
 
-def forward(waves, long, twiddle, short_hi, short_lo, high_ref, low_ref):
+def forward(waves, long, twiddle, short_hi, short_lo, high_ref, low_ref, pending=()):
     left, right = slice(0, LANES), slice(LANES, 2 * LANES)
     half = ROWS // 2
     spectra = []
     for wave in waves:
         fore = dot(long[:, :ROWS], jnp.concatenate([wave[:half], wave[:half]], axis=0))
         rear = dot(long[:, ROWS:], jnp.concatenate([wave[half:], wave[half:]], axis=0))
-        first = fore + 0.5 * rear
+        first = fore - rear
         done = len(spectra)
         for c in range(2):
             at = channel_rows(done + c)
@@ -80,6 +77,8 @@
             cosine, sine = twiddle[:, left], twiddle[:, right]
             store_halves(real * cosine - imag * sine, (at, left), high_ref, low_ref)
             store_halves(real * sine + imag * cosine, (at, right), high_ref, low_ref)
+        for copy in pending:
+            copy.wait()
         for c in range(2):
             spectra.append(times_short(high_ref, low_ref, channel_rows(done + c), short_hi, short_lo))
     return spectra
@@ -107,8 +106,7 @@
         table = jnp.concatenate([long[top, both], long[end, both], long[top, high], long[end, high]], axis=1)
         waves = [wide_hi[real], wide_hi[real], wide_hi[imag], wide_hi[imag], wide_lo[real], wide_lo[imag]]
         total.append(dot(table, jnp.concatenate(waves, axis=0)))
-    scale = 1.0 / (ROWS * LANES)
-    return total[0] * scale + total[1] * (0.5 * scale)
+    return (total[0] - total[1]) * (1.0 / (ROWS * LANES))
 
 
 def wave_of(ref, first):
@@ -150,10 +148,14 @@
 
 
 def correlate_body(
-    in_ref, long, twiddle, short_hi, short_lo, out_ref, high_ref, low_ref, wide_hi, wide_lo, scratch
+    in_ref, long, twiddle, short_hi, short_lo, out_ref, next_hbm,
+    high_ref, low_ref, wide_hi, wide_lo, scratch, next_spectra, semaphores,
 ):
-    waves = wave_of(in_ref, 0), wave_of(in_ref, 2)
+    waves = [wave_of(in_ref, 2 * i) for i in range(3)]
     spectra = forward(waves, long, twiddle, short_hi, short_lo, high_ref, low_ref)
+    for c in range(2):
+        next_spectra[channel_rows(c), :] = spectra[4 + c]
+    copies = fetch([next_spectra], [next_hbm], semaphores)
     products = []
     for c in range(2):
         s_re, s_im = spectra[c][:, :LANES], spectra[c][:, LANES:]
@@ -163,9 +165,10 @@
     for c in range(2):
         scratch[pl.ds(c, ROWS, stride=2), :] = result[:, channel_lanes(c)]
     out_ref[...] = scratch[...].astype(bf16).reshape(out_ref.shape)
-
-
-def adam_body(grad_ref, master, one, two, new_master, new_one, new_two, filters, rounded, semaphores):
+    copies[0].wait()
+
+
+def adam_body(grad_ref, master, one, two, new_master, new_one, new_two, filters):
     grad = grad_ref[0].astype(f32)
     for q in range(1, grad_ref.shape[0]):
         grad = grad + grad_ref[q].astype(f32)
@@ -175,42 +178,24 @@
     second_hat = second / (1.0 - 0.999**10)
     old = master[...]
     new = old - 0.01 * (first_hat / (jnp.sqrt(second_hat) + 1e-08) + 0.1 * old)
-    rounded[...] = new.astype(bf16)
-    owners = filters.shape[0]
-    copies = fetch([rounded] * owners, [filters.at[q] for q in range(owners)], semaphores)
     new_one[...] = first
     new_two[...] = second
     new_master[...] = new
-    for copy in copies:
-        copy.wait()
-
-
-def spectrum_body(in_ref, long, twiddle, short_hi, short_lo, out_ref, high_ref, low_ref, result, semaphores):
-    spectra = forward((wave_of(in_ref, 4),), long, twiddle, short_hi, short_lo, high_ref, low_ref)
-    for c in range(2):
-        result[channel_rows(c), :] = spectra[c]
-    for copy in fetch([result], [out_ref], semaphores):
-        copy.wait()
+    rounded = new.astype(bf16)
+    for q in range(filters.shape[0]):
+        filters[q] = rounded
 
 
 def convolve_body(
-    long, in_hbm, next_hbm, twiddle_hbm, short_hi_hbm, short_lo_hbm,
-    out_ref, high_ref, low_ref, wide_hi, wide_lo, scratch,
-    in_ref, next_ref, twiddle, short_hi, short_lo, semaphores,
+    in_ref, long, twiddle, short_hi, short_lo, next_hbm,
+    out_ref, high_ref, low_ref, wide_hi, wide_lo, scratch, next_ref, semaphores,
 ):
-    copies = fetch(
-        (in_hbm, twiddle_hbm, short_hi_hbm, short_lo_hbm, next_hbm),
-        (in_ref, twiddle, short_hi, short_lo, next_ref),
-        semaphores,
-    )
-    copies[0].wait()
+    copies = fetch([next_hbm], [next_ref], semaphores)
     scratch[...] = in_ref[...].reshape(2 * ROWS, LANES).astype(f32)
     wave = jnp.concatenate(
         [scratch[pl.ds(c, ROWS, stride=2), :].astype(bf16) for c in range(2)], axis=1
     )
-    for copy in copies[1:]:
-        copy.wait()
-    spectra = forward((wave,), long, twiddle, short_hi, short_lo, high_ref, low_ref)
+    spectra = forward((wave,), long, twiddle, short_hi, short_lo, high_ref, low_ref, copies)
     products = []
     for c in range(2):
         f_re, f_im = spectra[c][:, :LANES], spectra[c][:, LANES:]
@@ -270,7 +255,6 @@
     long, twiddle, short_hi, short_lo = (jnp.asarray(t) for t in tables())
     ahead = (long, twiddle, short_hi, short_lo)
     wide = [pltpu.VMEM((2 * ROWS, 2 * LANES), bf16)] * 2
-    tall = [pltpu.VMEM((4 * ROWS, 2 * LANES), bf16)] * 2
     narrow = [pltpu.VMEM((2 * ROWS, LANES), f32)]
 
     sources = (inputs[0], out_grad[0], next_inputs[0])
@@ -280,27 +264,22 @@
         + [pltpu.SemaphoreType.DMA((3,))],
         far=sources,
     )
-    waves = exchange(packed, "ctx")
     own = (2 * ROWS // owners, LANES)
-    (partial,) = call(
-        correlate_body, "correlate", (shape((owners, *own), bf16),), tall + wide + narrow, waves, *ahead
+    spectra = (2 * ROWS, 2 * LANES)
+    partial, next_spectrum = call(
+        correlate_body, "correlate", (shape((owners, *own), bf16), shape(spectra, f32)),
+        [pltpu.VMEM((6 * ROWS, 2 * LANES), bf16)] * 2 + wide + narrow
+        + [pltpu.VMEM(spectra, f32), pltpu.SemaphoreType.DMA((1,))],
+        exchange(packed, "ctx"), *ahead, far_out=True,
     )
     new_master, new_one, new_two, filters = call(
-        adam_body, "adam", (shape(own, f32),) * 3 + (shape((owners, *own), bf16),),
-        [pltpu.VMEM(own, bf16), pltpu.SemaphoreType.DMA((owners,))],
-        exchange(partial, "dp"), interleave(master), interleave(moment_one), interleave(moment_two), far_out=True,
-    )
-    spectra = (2 * ROWS, 2 * LANES)
-    (next_spectrum,) = call(
-        spectrum_body, "spectrum", (shape(spectra, f32),),
-        wide + [pltpu.VMEM(spectra, f32), pltpu.SemaphoreType.DMA((1,))], waves, *ahead, far_out=True,
-    )
-    far = (exchange(filters, "dp"), next_spectrum, twiddle, short_hi, short_lo)
+        adam_body, "adam", (shape(own, f32),) * 3 + (shape((owners, *own), bf16),), [],
+        exchange(partial, "dp"), interleave(master), interleave(moment_one), interleave(moment_two),
+    )
     (result,) = call(
         convolve_body, "convolve", (shape((peers, 2, pieces, LANES), bf16),),
-        wide + wide + narrow + [pltpu.VMEM(t.shape, t.dtype) for t in far]
-        + [pltpu.SemaphoreType.DMA((len(far),))],
-        long, far=far,
+        wide + wide + narrow + [pltpu.VMEM(spectra, f32), pltpu.SemaphoreType.DMA((1,))],
+        exchange(filters, "dp"), *ahead, far=(next_spectrum,),
     )
     (next_out,) = call(
         unpack_body, "unpack", (shape((channels, length), bf16),), [pltpu.VMEM((rows, LANES), f32)],

time: 91.5 us -> 89.2 us (0.975)
  blocking collectives: 65.4 us -> 75.5 us
  waiting for transfers between devices: 4.41 us -> 0 us
  starting transfers between devices: 4.07 us -> 0 us
  Pallas kernels: 15.7 us -> 12.6 us
    all_to_all x3 -> x4, blocking collectives: 65.4 us -> 75.5 us  [exchange(): return lax.all_to_all(values, axis, split_axis=0, concat_axis=0, tiled=True)]
    all_to_all x1 -> x0, waiting for transfers between devices: 4.41 us -> none  [exchange(): return lax.all_to_all(values, axis, split_axis=0, concat_axis=0, tiled=True)]
    all_to_all x1 -> x0, starting transfers between devices: 4.07 us -> none  [exchange(): return lax.all_to_all(values, axis, split_axis=0, concat_axis=0, tiled=True)]
    pallas_call x6 -> x5, Pallas kernels: 15.7 us -> 12.6 us  [call(): pl.pallas_call(body, out_shape=out_shape, in_specs=[inside] * len(near) +...]
  transfers between devices with their start and end apart: 1 -> 0, of which waited for: 1 -> 0; matrix products, arithmetic and copies ran while one was open for 0% -> 0% of each run, Pallas kernels for 3% -> 0%
where the time goes in v4:
time: 89.2 us; the launch traced here: 88.9 us
  blocking collectives  75.5 us (85%)
  Pallas kernels  12.6 us (14%)
    all_to_all x4, blocking collectives, exchange(): return lax.all_to_all(values, axis, split_axis=0, concat_axis=0, tiled=True)  75.5 us
    pallas_call x5, Pallas kernels, call(): pl.pallas_call(body, out_shape=out_shape, in_specs=[inside] * len(near) +...  12.6 us

profile of v4, /device:TPU:1, one launch (start us, length us, event | category | flops | bytes accessed | tf_op | source)
XLA Modules:
  0.0 88.9 jit_solution(17949298655966918362)
XLA Ops:
  0.6 0.0 copy-start.2
  0.6 0.0 copy-start.3
  0.7 0.0 copy-start.1
  0.7 0.0 copy-start
  0.7 2.0 %pack.1 = bf16[32,6,16,128]{3,2,1,0:T(8,128)(2,1)S(1)} custom-call(bf16[64,2048]{1,0:T(8,128)(2,1)} %bitcast.38, bf16[64,2048]{1,0:T(8,128)(2,1)} %bitcast.39, bf16[64,2048]{1,0:T(8,128)(2,1)} %bitcast.40), custom_call_target="tpu_custom_call" | custom-call | tf_op jit(solution)/shard_map/pack/pallas_call | solution.py:219
  2.6 32.1 %all_to_all.20.in_ref = bf16[32,6,16,128]{3,2,1,0:T(8,128)(2,1)S(1)} all-to-all(bf16[32,6,16,128]{3,2,1,0:T(8,128)(2,1)S(1)} %pack.1), channel_id=1, replica_groups=mesh['dp'=8,'ctx'=32] {'ctx'}, dimensions={0} | all-to-all | bytes 1572864 | tf_op jit(solution)/shard_map/all_to_all | solution.py:246
  34.8 0.0 copy-done.2
  34.8 0.0 copy-done.3
  34.8 0.0 copy-done.1
  34.8 0.0 copy-done
  34.8 0.0 copy-start.4
  34.8 0.0 copy-start.5
  34.8 0.0 copy-start.6
  34.8 5.5 %correlate.1 = (bf16[8,128,128]{2,1,0:T(8,128)(2,1)S(1)}, f32[1024,256]{1,0:T(8,128)}) custom-call(bf16[32,6,16,128]{3,2,1,0:T(8,128)(2,1)S(1)} %all_to_all.20.in_ref, bf16[1024,1024]{1,0:T(8,128)(2,1)S(1)} %copy-done, f32[512,256]{1,0:T(8,128)S(1)} %copy-done.1, bf16[256,256]{1,0:T(8,128)(2,1)S(1)} %copy-done.3, bf16[256,256]{1,0:T(8,128)(2,1)S(1)} %copy-done.2), custom_call_target="tpu_custom_call" | custom-call | tf_op jit(solution)/shard_map/correlate/pallas_call | solution.py:219
  40.3 13.8 %all_to_all.21.grad_ref = bf16[8,128,128]{2,1,0:T(8,128)(2,1)S(1)} all-to-all(bf16[8,128,128]{2,1,0:T(8,128)(2,1)S(1)} %get-tuple-element.10), channel_id=1, replica_groups=mesh['dp'=8,'ctx'=32] {'dp'}, dimensions={0} | all-to-all | bytes 524288 | tf_op jit(solution)/shard_map/all_to_all | solution.py:246
  54.1 0.0 copy-done.4
  54.1 0.0 copy-done.5
  54.1 0.0 copy-done.6
  54.1 0.7 adam.1
  54.9 10.0 %all_to_all.22.in_ref = bf16[8,128,128]{2,1,0:T(8,128)(2,1)S(1)} all-to-all(bf16[8,128,128]{2,1,0:T(8,128)(2,1)S(1)} %get-tuple-element.14), channel_id=1, replica_groups=mesh['dp'=8,'ctx'=32] {'dp'}, dimensions={0} | all-to-all | bytes 524288 | tf_op jit(solution)/shard_map/all_to_all | solution.py:246
  64.9 3.6 %convolve.1 = bf16[32,2,16,128]{3,2,1,0:T(8,128)(2,1)S(1)} custom-call(bf16[8,128,128]{2,1,0:T(8,128)(2,1)S(1)} %all_to_all.22.in_ref, bf16[1024,1024]{1,0:T(8,128)(2,1)S(1)} %copy-done, f32[512,256]{1,0:T(8,128)S(1)} %copy-done.1, bf16[256,256]{1,0:T(8,128)(2,1)S(1)} %copy-done.3, bf16[256,256]{1,0:T(8,128)(2,1)S(1)} %copy-done.2, ...), custom_call_target="tpu_custom_call" | custom-call | tf_op jit(solution)/shard_map/convolve/pallas_call | solution.py:219
  68.5 19.5 %all_to_all.23.in_ref = bf16[32,2,16,128]{3,2,1,0:T(8,128)(2,1)S(1)} all-to-all(bf16[32,2,16,128]{3,2,1,0:T(8,128)(2,1)S(1)} %convolve.1), channel_id=1, replica_groups=mesh['dp'=8,'ctx'=32] {'ctx'}, dimensions={0} | all-to-all | bytes 524288 | tf_op jit(solution)/shard_map/all_to_all | solution.py:246
  88.0 0.9 %unpack.1 = bf16[64,2048]{1,0:T(8,128)(2,1)} custom-call(bf16[32,2,16,128]{3,2,1,0:T(8,128)(2,1)S(1)} %all_to_all.23.in_ref), custom_call_target="tpu_custom_call" | custom-call | tf_op jit(solution)/shard_map/unpack/pallas_call | solution.py:219
Async XLA Ops:
  0.6 34.1 %copy-start.2 = (bf16[256,256]{1,0:T(8,128)(2,1)S(1)}, bf16[256,256]{1,0:T(8,128)(2,1)}, u32[]{:S(2)}) copy-start(bf16[256,256]{1,0:T(8,128)(2,1)} %constant.11.clone.short_lo) | copy-start | bytes 393220
  0.6 34.1 %copy-start.3 = (bf16[256,256]{1,0:T(8,128)(2,1)S(1)}, bf16[256,256]{1,0:T(8,128)(2,1)}, u32[]{:S(2)}) copy-start(bf16[256,256]{1,0:T(8,128)(2,1)} %constant.10.clone.short_hi) | copy-start | bytes 393220
  0.7 34.1 %copy-start.1 = (f32[512,256]{1,0:T(8,128)S(1)}, f32[512,256]{1,0:T(8,128)}, u32[]{:S(2)}) copy-start(f32[512,256]{1,0:T(8,128)} %constant.9.clone.twiddle) | copy-start | bytes 1572868
  0.7 34.1 %copy-start = (bf16[1024,1024]{1,0:T(8,128)(2,1)S(1)}, bf16[1024,1024]{1,0:T(8,128)(2,1)}, u32[]{:S(2)}) copy-start(bf16[1024,1024]{1,0:T(8,128)(2,1)} %constant.8.clone.long) | copy-start | bytes 6291460
  34.8 19.3 %copy-start.4 = (f32[2,8192]{1,0:T(2,128)S(1)}, f32[2,8192]{1,0:T(2,128)}, u32[]{:S(2)}) copy-start(f32[2,8192]{1,0:T(2,128)} %param.12) | copy-start | bytes 196612
  34.8 19.3 %copy-start.5 = (f32[2,8192]{1,0:T(2,128)S(1)}, f32[2,8192]{1,0:T(2,128)}, u32[]{:S(2)}) copy-start(f32[2,8192]{1,0:T(2,128)} %param.13) | copy-start | bytes 196612
  34.8 19.3 %copy-start.6 = (f32[2,8192]{1,0:T(2,128)S(1)}, f32[2,8192]{1,0:T(2,128)}, u32[]{:S(2)}) copy-start(f32[2,8192]{1,0:T(2,128)} %param.14) | copy-start | bytes 196612

commit v5 on v4

--- a/solution.py
+++ b/solution.py
@@ -66,21 +66,23 @@
     left, right = slice(0, LANES), slice(LANES, 2 * LANES)
     half = ROWS // 2
     spectra = []
+    firsts = []
     for wave in waves:
         fore = dot(long[:, :ROWS], jnp.concatenate([wave[:half], wave[:half]], axis=0))
         rear = dot(long[:, ROWS:], jnp.concatenate([wave[half:], wave[half:]], axis=0))
-        first = fore - rear
-        done = len(spectra)
+        firsts.append(fore - rear)
+    for w, first in enumerate(firsts):
         for c in range(2):
-            at = channel_rows(done + c)
+            at = channel_rows(2 * w + c)
             real, imag = first[:ROWS, channel_lanes(c)], first[ROWS:, channel_lanes(c)]
             cosine, sine = twiddle[:, left], twiddle[:, right]
             store_halves(real * cosine - imag * sine, (at, left), high_ref, low_ref)
             store_halves(real * sine + imag * cosine, (at, right), high_ref, low_ref)
-        for copy in pending:
-            copy.wait()
+    for copy in pending:
+        copy.wait()
+    for w in range(len(waves)):
         for c in range(2):
-            spectra.append(times_short(high_ref, low_ref, channel_rows(done + c), short_hi, short_lo))
+            spectra.append(times_short(high_ref, low_ref, channel_rows(2 * w + c), short_hi, short_lo))
     return spectra
 
 
@@ -133,18 +135,30 @@
     for i in range(count):
         copies[i].wait()
         channels = arrived[i].shape[0]
+        pitch = pieces + 1
         for k in range(pieces):
             lanes = slice(k * LANES, (k + 1) * LANES)
-            scratch[i][pl.ds(k, channels, stride=pieces), :] = arrived[i][:, lanes].astype(f32)
-        out_ref[:, 2 * i : 2 * i + 2] = scratch[i][...].reshape(peers, 2, pieces, LANES).astype(bf16)
-
-
-def unpack_body(in_ref, out_ref, scratch):
-    channels, length = out_ref.shape
+            scratch[i][pl.ds(k, channels, stride=pitch), :] = arrived[i][:, lanes].astype(f32)
+        for c in range(channels):
+            out_ref[c // 2, 2 * i + c % 2] = scratch[i][c * pitch : c * pitch + pieces, :].astype(bf16)
+
+
+def unpack_body(in_ref, out_hbm, scratch, result, semaphores):
+    channels, length = out_hbm.shape
     pieces = length // LANES
-    scratch[...] = in_ref[...].astype(f32).reshape(channels * pieces, LANES)
-    for k in range(pieces):
-        out_ref[:, k * LANES : (k + 1) * LANES] = scratch[pl.ds(k, channels, stride=pieces), :].astype(bf16)
+    pitch = pieces + 1
+    group = 16
+    copies = []
+    for start in range(0, channels, group):
+        for c in range(start, start + group):
+            scratch[c * pitch : c * pitch + pieces, :] = in_ref[c // 2, c % 2].astype(f32)
+        rows = pl.ds(start, group)
+        for k in range(pieces):
+            lanes = slice(k * LANES, (k + 1) * LANES)
+            result[rows, lanes] = scratch[pl.ds(start * pitch + k, group, stride=pitch), :].astype(bf16)
+        copies += fetch([result.at[rows]], [out_hbm.at[rows]], semaphores.at[pl.ds(start // group, 1)])
+    for copy in copies:
+        copy.wait()
 
 
 def correlate_body(
@@ -260,7 +274,7 @@
     sources = (inputs[0], out_grad[0], next_inputs[0])
     (packed,) = call(
         pack_body, "pack", (shape((peers, 6, pieces, LANES), bf16),),
-        [pltpu.VMEM((channels, length), bf16)] * 3 + [pltpu.VMEM((rows, LANES), f32)] * 3
+        [pltpu.VMEM((channels, length), bf16)] * 3 + [pltpu.VMEM((rows + channels, LANES), f32)] * 3
         + [pltpu.SemaphoreType.DMA((3,))],
         far=sources,
     )
@@ -282,8 +296,10 @@
         exchange(filters, "dp"), *ahead, far=(next_spectrum,),
     )
     (next_out,) = call(
-        unpack_body, "unpack", (shape((channels, length), bf16),), [pltpu.VMEM((rows, LANES), f32)],
-        exchange(result, "ctx"),
+        unpack_body, "unpack", (shape((channels, length), bf16),),
+        [pltpu.VMEM((rows + channels, LANES), f32), pltpu.VMEM((channels, length), bf16)]
+        + [pltpu.SemaphoreType.DMA((channels // 16,))],
+        exchange(result, "ctx"), far_out=True,
     )
     return (deinterleave(new_master, 2), deinterleave(new_one, 2), deinterleave(new_two, 2), next_out[None])
 

time: 89.2 us -> 87.8 us (0.984)
  Pallas kernels: 12.6 us -> 11.3 us
    pallas_call x5, Pallas kernels: 12.6 us -> 11.3 us  [call(): pl.pallas_call(body, out_shape=out_shape, in_specs=[inside] * len(near) +...]
where the time goes in v5:
time: 87.8 us; the launch traced here: 87.6 us
  blocking collectives  75.5 us (86%)
  Pallas kernels  11.3 us (13%)
    all_to_all x4, blocking collectives, exchange(): return lax.all_to_all(values, axis, split_axis=0, concat_axis=0, tiled=True)  75.5 us
    pallas_call x5, Pallas kernels, call(): pl.pallas_call(body, out_shape=out_shape, in_specs=[inside] * len(near) +...  11.3 us

profile of v5, /device:TPU:1, one launch (start us, length us, event | category | flops | bytes accessed | tf_op | source)
XLA Modules:
  0.0 87.6 jit_solution(17301876828459668461)
XLA Ops:
  0.6 0.0 copy-start.2
  0.6 0.0 copy-start.3
  0.7 0.0 copy-start.1
  0.7 0.0 copy-start
  0.7 1.3 %pack.1 = bf16[32,6,16,128]{3,2,1,0:T(8,128)(2,1)S(1)} custom-call(bf16[64,2048]{1,0:T(8,128)(2,1)} %bitcast.38, bf16[64,2048]{1,0:T(8,128)(2,1)} %bitcast.39, bf16[64,2048]{1,0:T(8,128)(2,1)} %bitcast.40), custom_call_target="tpu_custom_call" | custom-call | tf_op jit(solution)/shard_map/pack/pallas_call | solution.py:233
  2.0 32.1 %all_to_all.20.in_ref = bf16[32,6,16,128]{3,2,1,0:T(8,128)(2,1)S(1)} all-to-all(bf16[32,6,16,128]{3,2,1,0:T(8,128)(2,1)S(1)} %pack.1), channel_id=1, replica_groups=mesh['dp'=8,'ctx'=32] {'ctx'}, dimensions={0} | all-to-all | bytes 1572864 | tf_op jit(solution)/shard_map/all_to_all | solution.py:260
  34.2 0.0 copy-done.2
  34.2 0.0 copy-done.3
  34.2 0.0 copy-done.1
  34.2 0.0 copy-done
  34.2 0.0 copy-start.4
  34.2 0.0 copy-start.5
  34.2 0.0 copy-start.6
  34.2 4.9 %correlate.1 = (bf16[8,128,128]{2,1,0:T(8,128)(2,1)S(1)}, f32[1024,256]{1,0:T(8,128)}) custom-call(bf16[32,6,16,128]{3,2,1,0:T(8,128)(2,1)S(1)} %all_to_all.20.in_ref, bf16[1024,1024]{1,0:T(8,128)(2,1)S(1)} %copy-done, f32[512,256]{1,0:T(8,128)S(1)} %copy-done.1, bf16[256,256]{1,0:T(8,128)(2,1)S(1)} %copy-done.3, bf16[256,256]{1,0:T(8,128)(2,1)S(1)} %copy-done.2), custom_call_target="tpu_custom_call" | custom-call | tf_op jit(solution)/shard_map/correlate/pallas_call | solution.py:233
  39.1 13.8 %all_to_all.21.grad_ref = bf16[8,128,128]{2,1,0:T(8,128)(2,1)S(1)} all-to-all(bf16[8,128,128]{2,1,0:T(8,128)(2,1)S(1)} %get-tuple-element.10), channel_id=1, replica_groups=mesh['dp'=8,'ctx'=32] {'dp'}, dimensions={0} | all-to-all | bytes 524288 | tf_op jit(solution)/shard_map/all_to_all | solution.py:260
  52.9 0.0 copy-done.4
  52.9 0.0 copy-done.5
  52.9 0.0 copy-done.6
  52.9 0.7 adam.1
  53.7 10.0 %all_to_all.22.in_ref = bf16[8,128,128]{2,1,0:T(8,128)(2,1)S(1)} all-to-all(bf16[8,128,128]{2,1,0:T(8,128)(2,1)S(1)} %get-tuple-element.14), channel_id=1, replica_groups=mesh['dp'=8,'ctx'=32] {'dp'}, dimensions={0} | all-to-all | bytes 524288 | tf_op jit(solution)/shard_map/all_to_all | solution.py:260
  63.7 3.6 %convolve.1 = bf16[32,2,16,128]{3,2,1,0:T(8,128)(2,1)S(1)} custom-call(bf16[8,128,128]{2,1,0:T(8,128)(2,1)S(1)} %all_to_all.22.in_ref, bf16[1024,1024]{1,0:T(8,128)(2,1)S(1)} %copy-done, f32[512,256]{1,0:T(8,128)S(1)} %copy-done.1, bf16[256,256]{1,0:T(8,128)(2,1)S(1)} %copy-done.3, bf16[256,256]{1,0:T(8,128)(2,1)S(1)} %copy-done.2, ...), custom_call_target="tpu_custom_call" | custom-call | tf_op jit(solution)/shard_map/convolve/pallas_call | solution.py:233
  67.3 19.5 %all_to_all.23.in_ref = bf16[32,2,16,128]{3,2,1,0:T(8,128)(2,1)S(1)} all-to-all(bf16[32,2,16,128]{3,2,1,0:T(8,128)(2,1)S(1)} %convolve.1), channel_id=1, replica_groups=mesh['dp'=8,'ctx'=32] {'ctx'}, dimensions={0} | all-to-all | bytes 524288 | tf_op jit(solution)/shard_map/all_to_all | solution.py:260
  86.8 0.8 unpack.1
Async XLA Ops:
  0.6 33.5 %copy-start.2 = (bf16[256,256]{1,0:T(8,128)(2,1)S(1)}, bf16[256,256]{1,0:T(8,128)(2,1)}, u32[]{:S(2)}) copy-start(bf16[256,256]{1,0:T(8,128)(2,1)} %constant.11.clone.short_lo) | copy-start | bytes 393220
  0.6 33.5 %copy-start.3 = (bf16[256,256]{1,0:T(8,128)(2,1)S(1)}, bf16[256,256]{1,0:T(8,128)(2,1)}, u32[]{:S(2)}) copy-start(bf16[256,256]{1,0:T(8,128)(2,1)} %constant.10.clone.short_hi) | copy-start | bytes 393220
  0.7 33.5 %copy-start.1 = (f32[512,256]{1,0:T(8,128)S(1)}, f32[512,256]{1,0:T(8,128)}, u32[]{:S(2)}) copy-start(f32[512,256]{1,0:T(8,128)} %constant.9.clone.twiddle) | copy-start | bytes 1572868
  0.7 33.5 %copy-start = (bf16[1024,1024]{1,0:T(8,128)(2,1)S(1)}, bf16[1024,1024]{1,0:T(8,128)(2,1)}, u32[]{:S(2)}) copy-start(bf16[1024,1024]{1,0:T(8,128)(2,1)} %constant.8.clone.long) | copy-start | bytes 6291460
  34.2 18.7 %copy-start.4 = (f32[2,8192]{1,0:T(2,128)S(1)}, f32[2,8192]{1,0:T(2,128)}, u32[]{:S(2)}) copy-start(f32[2,8192]{1,0:T(2,128)} %param.12) | copy-start | bytes 196612
  34.2 18.7 %copy-start.5 = (f32[2,8192]{1,0:T(2,128)S(1)}, f32[2,8192]{1,0:T(2,128)}, u32[]{:S(2)}) copy-start(f32[2,8192]{1,0:T(2,128)} %param.13) | copy-start | bytes 196612
  34.2 18.7 %copy-start.6 = (f32[2,8192]{1,0:T(2,128)S(1)}, f32[2,8192]{1,0:T(2,128)}, u32[]{:S(2)}) copy-start(f32[2,8192]{1,0:T(2,128)} %param.14) | copy-start | bytes 196612
